TPU v7x, 512 devices: a whole 4x8x8 slice. The times are simulated.
512 devices in a mesh: dp: 4 (over x), expert: 128 (over z, y, core).
Axes of the slice: x: 4, y: 8, z: 8, core: 2. Of those that a mesh axis runs over, the one named last changes fastest.
Arguments:
- tokens: bfloat16 [8192, 2048], P(('dp', 'expert')), may hold values from -6 to 6
- cotangent: bfloat16 [8192, 2048], P(('dp', 'expert')), may hold values from -6 to 6
- routes: int32 [8192, 8], P(('dp', 'expert')), may hold values from 0 to 127, all different within a row; in each aligned block of 16 rows (0 to 15, 16 to 31, ...) at most 2 rows name the same one
- gate_values: float32 [8192, 8], P(('dp', 'expert')), may hold values from 0.1 to 1
- gate_weight: bfloat16 [128, 768, 2048], P('expert', 'dp'), may hold values from -0.125 to 0.125
- up_weight: bfloat16 [128, 768, 2048], P('expert', 'dp'), may hold values from -0.125 to 0.125
- down_weight: bfloat16 [128, 768, 2048], P('expert', None, 'dp'), may hold values from -0.21875 to 0.21875
Outputs:
- mixed: bfloat16 [8192, 2048], P(('dp', 'expert'))
- grad_gate_weight: bfloat16 [128, 768, 2048], P('expert', 'dp')
- grad_up_weight: bfloat16 [128, 768, 2048], P('expert', 'dp')
- grad_down_weight: bfloat16 [128, 768, 2048], P('expert', None, 'dp')
Inputs may be any that keep to these rules, and one draw needn't show every extreme that they name: `routes`: each row names 8 different experts. Among the rows of one device no expert is named more than 2 times, and in some device's rows some expert is named exactly 2 times.
All inputs are finite; a program needn't handle non-finite values.
Results may differ from a plain program's by a relative error of at most 0.0058.
Values may be sent and summed in bfloat16 or wider, within the bound.
A program may use at most 64 MiB of HBM per device.

v0:
```python
import jax
import jax.numpy as jnp
from jax import lax
from jax.sharding import PartitionSpec as P


def body(tokens, cotangent, routes, gate_values, gate_weight, up_weight, down_weight):
    tok_rows = tokens.shape[0]
    width = tokens.shape[1]
    top_count = routes.shape[1]
    experts = lax.axis_size("expert")
    groups = lax.axis_size("dp")
    capacity = min(tok_rows, max(2, 2 * tok_rows * top_count // experts))
    onehot = routes[:, :, None] == jnp.arange(experts, dtype=jnp.int32)[None, None, :]
    named = jnp.sum(onehot.astype(jnp.int32), axis=1)
    earlier = jnp.cumsum(named, axis=0) - named
    slot_ids = jnp.arange(capacity, dtype=jnp.int32)[None, :, None]
    placer = (named.T[:, None, :] == 1) & (earlier.T[:, None, :] == slot_ids)
    placer_half = placer.astype(jnp.bfloat16)
    placer_full = placer.astype(jnp.float32)
    token_gate = jnp.sum(
        jnp.where(onehot, gate_values[:, :, None], jnp.zeros((), jnp.float32)), axis=1
    )
    slot_gate = jnp.sum(placer_full * token_gate.T[:, None, :], axis=2)
    row_input = jnp.einsum(
        "est,td->esd", placer_half, tokens, preferred_element_type=jnp.float32
    ).astype(jnp.bfloat16)
    picked_cot = jnp.einsum(
        "est,td->esd", placer_half, cotangent, preferred_element_type=jnp.float32
    )
    row_cot = (slot_gate[:, :, None] * picked_cot).astype(jnp.bfloat16)
    arrived_input, arrived_cot = (
        lax.all_to_all(row_input, "expert", split_axis=0, concat_axis=0, tiled=True),
        lax.all_to_all(row_cot, "expert", split_axis=0, concat_axis=0, tiled=True),
    )
    local_rows = arrived_input.shape[0] * arrived_input.shape[1]
    flat_input = arrived_input.reshape(local_rows, width)
    flat_cot = arrived_cot.reshape(local_rows, width)
    gate_local = gate_weight[0]
    up_local = up_weight[0]
    down_local = down_weight[0]
    quarter_width = down_local.shape[1]
    inputs_all = lax.all_gather(flat_input, "dp", axis=0, tiled=True)
    cot_quarter = lax.all_to_all(flat_cot, "dp", split_axis=1, concat_axis=0, tiled=True)
    contract_last = (((1,), (1,)), ((), ()))
    gate_pre = lax.dot_general(
        gate_local, inputs_all, contract_last, preferred_element_type=jnp.float32
    )
    up_pre = lax.dot_general(
        up_local, inputs_all, contract_last, preferred_element_type=jnp.float32
    )
    hidden_part = (jax.nn.silu(gate_pre) * up_pre).astype(jnp.bfloat16)
    hidden_all = lax.all_gather(hidden_part, "dp", axis=0, tiled=True)
    contract_lead = (((0,), (0,)), ((), ()))
    expert_out = lax.dot_general(
        hidden_all, down_local, contract_lead, preferred_element_type=jnp.float32
    ).astype(jnp.bfloat16)
    grad_down = jnp.dot(hidden_all, cot_quarter, preferred_element_type=jnp.float32).astype(
        jnp.bfloat16
    )
    grad_hidden = lax.psum_scatter(
        lax.dot_general(down_local, cot_quarter, contract_last, preferred_element_type=jnp.float32),
        "dp",
        scatter_dimension=0,
        tiled=True,
    )
    sigma = jax.nn.sigmoid(gate_pre)
    grad_gate = (grad_hidden * up_pre * sigma * (1.0 + gate_pre * (1.0 - sigma))).astype(
        jnp.bfloat16
    )
    grad_up = (grad_hidden * jax.nn.silu(gate_pre)).astype(jnp.bfloat16)
    grad_gate_local = jnp.dot(grad_gate, inputs_all, preferred_element_type=jnp.float32).astype(
        jnp.bfloat16
    )
    grad_up_local = jnp.dot(grad_up, inputs_all, preferred_element_type=jnp.float32).astype(
        jnp.bfloat16
    )
    out_blocks = expert_out.reshape(groups, experts, capacity, quarter_width)
    returned = lax.all_to_all(
        lax.all_to_all(out_blocks, "dp", split_axis=0, concat_axis=3, tiled=True),
        "expert",
        split_axis=1,
        concat_axis=1,
        tiled=True,
    )
    returned_rows = returned.reshape(experts * capacity, width).astype(jnp.float32)
    combine_rows = (placer_full * slot_gate[:, :, None]).reshape(experts * capacity, tok_rows)
    mixed = lax.dot_general(
        combine_rows,
        returned_rows,
        contract_lead,
        precision=lax.Precision.HIGHEST,
        preferred_element_type=jnp.float32,
    ).astype(jnp.bfloat16)
    return (mixed, grad_gate_local[None], grad_up_local[None], grad_down[None])


def solution(mesh):
    in_specs = (
        P(("dp", "expert"), None),
        P(("dp", "expert"), None),
        P(("dp", "expert"), None),
        P(("dp", "expert"), None),
        P("expert", "dp", None),
        P("expert", "dp", None),
        P("expert", None, "dp"),
    )
    out_specs = (
        P(("dp", "expert"), None),
        P("expert", "dp", None),
        P("expert", "dp", None),
        P("expert", None, "dp"),
    )
    return jax.shard_map(body, mesh=mesh, in_specs=in_specs, out_specs=out_specs, check_vma=False)
```

profile of v0, /device:TPU:1, one launch (start us, length us, event | category | flops | bytes accessed | tf_op | source)
XLA Modules:
  0.0 236.6 jit_solution(17935731720747272963)
XLA Ops:
  9.8 1.3 convolution_convert_fusion
  11.1 1.1 copy.59
  12.2 49.3 %all_to_all.52 = bf16[128,2,2048]{2,1,0:T(2,128)(2,1)S(1)} all-to-all(bf16[128,2,2048]{2,1,0:T(2,128)(2,1)S(1)} %copy.59), channel_id=1, replica_groups=mesh['dp'=4,'expert'=128] {'expert'}, dimensions={0} | all-to-all | bytes 2097152 | tf_op jit(solution)/shard_map/all_to_all | solution.py:33
  61.4 1.2 reshape.91
  63.2 2.1 copy.65
  65.3 6.5 %all-to-all-start.3 = ((bf16[128,2,2048]{2,1,0:T(2,128)(2,1)}), bf16[128,2,2048]{2,1,0:T(2,128)(2,1)S(1)}, u32[]{:S(2)}, u32[]{:S(2)}) async-start(bf16[128,2,2048]{2,1,0:T(2,128)(2,1)} %copy.65), calls=%async_computation.3 | async-start | bytes 2097152 | tf_op jit(solution)/shard_map/all_to_all | solution.py:34
  71.8 38.1 %all-gather.3.cloned.1.call-done = bf16[1024,2048]{1,0:T(8,128)(2,1)} async-done(((bf16[256,2048]{1,0:T(8,128)(2,1)}), bf16[1024,2048]{1,0:T(8,128)(2,1)}) %all-gather.3.cloned.1.call-update) | async-done | bytes 4194320 | tf_op jit(solution)/shard_map/all_gather | solution.py:43
  110.0 3.9 %convolution_bitcast_fusion.2 = f32[192,1024]{1,0:T(8,128)S(1)} fusion(bf16[1024,2048]{1,0:T(8,128)(2,1)} %all-gather.3.cloned.1.call-done, bf16[1,192,2048]{2,1,0:T(8,128)(2,1)S(1)} %copy-done.5), kind=kOutput, calls=%fused_computation.13 | convolution fusion | flops 805306368 | bytes 5767168 | tf_op jit(solution)/shard_map/dot_general | solution.py:46
  113.9 2.6 %multiply_convert_fusion.2 = (bf16[192,1024]{1,0:T(8,128)(2,1)}, f32[192,1024]{1,0:T(8,128)}) fusion(f32[192,1024]{1,0:T(8,128)S(1)} %convolution_bitcast_fusion.2, bf16[1024,2048]{1,0:T(8,128)(2,1)S(1)} %copy-done.2, bf16[1,192,2048]{2,1,0:T(8,128)(2,1)S(1)} %copy-done.6), kind=kOutput, calls=%fused_computation.20 | convolution fusion | flops 806486016 | bytes 6946816 | tf_op jit(solution)/shard_map/dot_general | solution.py:49
  117.5 17.0 %all_to_all.53 = bf16[256,4,512]{2,0,1:T(8,128)(2,1)S(1)} all-to-all(bf16[256,4,512]{2,0,1:T(8,128)(2,1)S(1)} %copy.66), channel_id=1, replica_groups=mesh['dp'=4,'expert'=128] {'dp'}, dimensions={1} | all-to-all | bytes 2097152 | tf_op jit(solution)/shard_map/all_to_all | solution.py:44
  134.5 2.7 %convolution_bitcast_fusion = f32[768,1024]{1,0:T(8,128)} fusion(bf16[1024,512]{1,0:T(8,128)(2,1)S(1)} %bitcast.59, bf16[1,768,512]{2,1,0:T(8,128)(2,1)S(1)} %copy-done), kind=kOutput, calls=%fused_computation.8 | convolution fusion | flops 805306368 | bytes 4980736 | tf_op jit(solution)/shard_map/dot_general | solution.py:62
  137.3 11.7 %all-gather.5.cloned.1.call-done = bf16[768,1024]{1,0:T(8,128)(2,1)} async-done(((bf16[192,1024]{1,0:T(8,128)(2,1)}), bf16[768,1024]{1,0:T(8,128)(2,1)}) %all-gather.5.cloned.1.call-update) | async-done | bytes 1572880 | tf_op jit(solution)/shard_map/all_gather | solution.py:53
  148.9 3.4 %convolution_convert_fusion.4 = bf16[1024,512]{1,0:T(8,128)(2,1)} fusion(bf16[768,1024]{1,0:T(8,128)(2,1)} %all-gather.5.cloned.1.call-done, bf16[1,768,512]{2,1,0:T(8,128)(2,1)S(1)} %copy-done), kind=kOutput, calls=%fused_computation.9 | convolution fusion | flops 805830656 | bytes 3407872 | tf_op jit(solution)/shard_map/dot_general | solution.py:55
  152.3 1.5 reshape.92
  153.8 2.0 copy.60
  155.8 21.9 %all_to_all.54 = bf16[4,128,2,512]{1,3,2,0:T(8,128)(2,1)S(1)} all-to-all(bf16[4,128,2,512]{1,3,2,0:T(8,128)(2,1)} %copy.60), channel_id=1, replica_groups=mesh['dp'=4,'expert'=128] {'dp'}, dimensions={0} | all-to-all | bytes 2097152 | tf_op jit(solution)/shard_map/all_to_all | solution.py:80
  177.7 2.1 copy.62
  179.8 17.7 %all-to-all-start.2 = ((bf16[1,128,2,2048]{3,2,0,1:T(2,128)(2,1)}), bf16[1,128,2,2048]{3,2,0,1:T(2,128)(2,1)S(1)}, u32[]{:S(2)}, u32[]{:S(2)}) async-start(bf16[1,128,2,2048]{3,2,0,1:T(2,128)(2,1)} %copy.62), calls=%async_computation.2 | async-start | bytes 2097152 | tf_op jit(solution)/shard_map/all_to_all | solution.py:79
  197.7 3.4 %reduce-scatter.2.cloned.1.call-done = f32[192,1024]{1,0:T(8,128)} async-done(((f32[768,1024]{1,0:T(8,128)}), f32[192,1024]{1,0:T(8,128)}) %reduce-scatter.2.cloned.1.call-update) | async-done | bytes 786448 | tf_op jit(solution)/shard_map/reduce_scatter | solution.py:61
  201.2 4.7 %fusion.2 = bf16[1,192,2048]{2,1,0:T(8,128)(2,1)} fusion(bf16[1024,2048]{1,0:T(8,128)(2,1)} %all-gather.3.cloned.1.call-done, f32[192,1024]{1,0:T(8,128)} %reduce-scatter.2.cloned.1.call-done, f32[192,1024]{1,0:T(8,128)} %copy-done.8), kind=kOutput, calls=%fused_computation.6 | convolution fusion | flops 806879232 | bytes 6553600 | tf_op jit(solution)/shard_map/dot_general | solution.py:75
  205.9 2.0 fusion.1
  208.0 1.9 fusion.3
  209.8 18.6 %all-to-all-done.2 = bf16[1,128,2,2048]{3,2,0,1:T(2,128)(2,1)S(1)} async-done(((bf16[1,128,2,2048]{3,2,0,1:T(2,128)(2,1)}), bf16[1,128,2,2048]{3,2,0,1:T(2,128)(2,1)S(1)}, u32[]{:S(2)}, u32[]{:S(2)}) %all-to-all-start.2) | async-done | bytes 1048608 | tf_op jit(solution)/shard_map/all_to_all | solution.py:79
  228.9 1.2 convolution_convert_fusion.3
  (48 shorter events, 4.9 us)
Async XLA Ops:
  7.2 127.4 %copy-start = (bf16[1,768,512]{2,1,0:T(8,128)(2,1)S(1)}, bf16[1,768,512]{2,1,0:T(8,128)(2,1)}, u32[]{:S(2)}) copy-start(bf16[1,768,512]{2,1,0:T(8,128)(2,1)} %param.13) | copy-start | bytes 2359300
  7.2 102.8 %all-gather.3.cloned.1.call-start = ((), (), s32[]{:S(2)}) async-start(), calls=%async_computation.6 | async-start | bytes 5242880 | tf_op jit(solution)/shard_map/all_gather | solution.py:43
  12.2 50.6 %copy-start.1 = (bf16[16,2048]{1,0:T(8,128)(2,1)S(1)}, bf16[16,2048]{1,0:T(8,128)(2,1)}, u32[]{:S(2)}) copy-start(bf16[16,2048]{1,0:T(8,128)(2,1)} %param.8) | copy-start | bytes 196612
  62.6 47.3 %copy-start.5 = (bf16[1,192,2048]{2,1,0:T(8,128)(2,1)S(1)}, bf16[1,192,2048]{2,1,0:T(8,128)(2,1)}, u32[]{:S(2)}) copy-start(bf16[1,192,2048]{2,1,0:T(8,128)(2,1)} %param.11) | copy-start | bytes 2359300
  65.3 51.3 %all-to-all-start.3 = ((bf16[128,2,2048]{2,1,0:T(2,128)(2,1)}), bf16[128,2,2048]{2,1,0:T(2,128)(2,1)S(1)}, u32[]{:S(2)}, u32[]{:S(2)}) async-start(bf16[128,2,2048]{2,1,0:T(2,128)(2,1)} %copy.65), calls=%async_computation.3 | async-start | bytes 2097152 | tf_op jit(solution)/shard_map/all_to_all | solution.py:34
  71.8 42.0 %copy-start.6 = (bf16[1,192,2048]{2,1,0:T(8,128)(2,1)S(1)}, bf16[1,192,2048]{2,1,0:T(8,128)(2,1)}, u32[]{:S(2)}) copy-start(bf16[1,192,2048]{2,1,0:T(8,128)(2,1)} %param.12) | copy-start | bytes 2359300
  71.8 77.1 %all-gather.5.cloned.1.call-start = ((), (), s32[]{:S(2)}) async-start(), calls=%async_computation.7 | async-start | bytes 1966080 | tf_op jit(solution)/shard_map/all_gather | solution.py:53
  110.0 3.9 %copy-start.2 = (bf16[1024,2048]{1,0:T(8,128)(2,1)S(1)}, bf16[1024,2048]{1,0:T(8,128)(2,1)}, u32[]{:S(2)}) copy-start(bf16[1024,2048]{1,0:T(8,128)(2,1)} %all-gather.3.cloned.1.call-done) | copy-start | bytes 12582916
  113.8 2.6 %copy-start.8 = (f32[192,1024]{1,0:T(8,128)}, f32[192,1024]{1,0:T(8,128)S(1)}, u32[]{:S(2)}) copy-start(f32[192,1024]{1,0:T(8,128)S(1)} %convolution_bitcast_fusion.2) | copy-start | bytes 2359300
  116.5 84.6 %reduce-scatter.2.cloned.1.call-start = ((), (), s32[]{:S(2)}) async-start(), calls=%async_computation.8 | async-start | bytes 3932160 | tf_op jit(solution)/shard_map/reduce_scatter | solution.py:61
  179.8 48.6 %all-to-all-start.2 = ((bf16[1,128,2,2048]{3,2,0,1:T(2,128)(2,1)}), bf16[1,128,2,2048]{3,2,0,1:T(2,128)(2,1)S(1)}, u32[]{:S(2)}, u32[]{:S(2)}) async-start(bf16[1,128,2,2048]{3,2,0,1:T(2,128)(2,1)} %copy.62), calls=%async_computation.2 | async-start | bytes 2097152 | tf_op jit(solution)/shard_map/all_to_all | solution.py:79
  201.2 4.7 %copy-start.3 = (bf16[1024,2048]{1,0:T(8,128)(2,1)S(1)}, bf16[1024,2048]{1,0:T(8,128)(2,1)}, u32[]{:S(2)}) copy-start(bf16[1024,2048]{1,0:T(8,128)(2,1)} %all-gather.3.cloned.1.call-done) | copy-start | bytes 12582916
  201.2 4.7 %copy-start.7 = (f32[192,1024]{1,0:T(8,128)S(1)}, f32[192,1024]{1,0:T(8,128)}, u32[]{:S(2)}) copy-start(f32[192,1024]{1,0:T(8,128)} %reduce-scatter.2.cloned.1.call-done) | copy-start | bytes 2359300
  201.2 4.7 %copy-start.9 = (f32[192,1024]{1,0:T(8,128)S(1)}, f32[192,1024]{1,0:T(8,128)}, u32[]{:S(2)}) copy-start(f32[192,1024]{1,0:T(8,128)} %copy-done.8) | copy-start | bytes 2359300
  201.2 4.7 %copy-start.10 = (f32[192,1024]{1,0:T(8,128)S(1)}, f32[192,1024]{1,0:T(8,128)}, u32[]{:S(2)}) copy-start(f32[192,1024]{1,0:T(8,128)} %get-tuple-element.7) | copy-start | bytes 2359300
  205.9 2.1 copy-start.4
Sparse Core Ops, SparseCore 0:
  62.8 47.1 all-gather.2
  116.6 32.2 all-gather.4
  151.8 49.3 reduce-scatter.1
where the time goes:
time: 237 us
  blocking collectives  88.2 us (37%)
  waiting for transfers between devices  71.9 us (30%)
  starting transfers between devices  24.3 us (10%)
  matrix products  24.2 us (10%)
  between operations  13.9 us (6%)
  local copies, waits for them, and re-layouts  13.4 us (6%)
    all_to_all x1, blocking collectives, body(): lax.all_to_all(row_input, 'expert', split_axis=0, concat_axis=0, tiled=True)  49.3 us
    all_gather x1, waiting for transfers between devices, body(): inputs_all = lax.all_gather(flat_input, 'dp', axis=0, tiled=True)  38.1 us
    all_to_all x1, blocking collectives, body(): lax.all_to_all(out_blocks, 'dp', split_axis=0, concat_axis=3, tiled=True)  21.9 us
    all_to_all x1, waiting for transfers between devices, body(): lax.all_to_all(lax.all_to_all(out_blocks, 'dp', split_axis=0, concat_axis...  18.6 us
    all_to_all x1, starting transfers between devices, body(): lax.all_to_all(lax.all_to_all(out_blocks, 'dp', split_axis=0, concat_axis...  17.7 us
    all_to_all x1, blocking collectives, body(): lax.all_to_all(flat_cot, 'dp', split_axis=1, concat_axis=0, tiled=True)  17 us
    all_gather x1, waiting for transfers between devices, body(): hidden_all = lax.all_gather(hidden_part, 'dp', axis=0, tiled=True)  11.7 us
    all_to_all x1, starting transfers between devices, body(): lax.all_to_all(row_cot, 'expert', split_axis=0, concat_axis=0, tiled=True)  6.48 us
  transfers between devices with their start and end apart: 5, of which 4 were waited for; matrix products, arithmetic and copies ran while one was open for 13% of the time, Pallas kernels for 0%

commit v1 on v0

v1 whole, which is shorter than its diff:
```python
import jax
import jax.numpy as jnp
from jax import lax
from jax.sharding import PartitionSpec as P


def placement(routes, gate_values, experts, capacity):
    onehot = routes[:, :, None] == jnp.arange(experts, dtype=jnp.int32)[None, None, :]
    named = jnp.sum(onehot.astype(jnp.int32), axis=1)
    earlier = jnp.cumsum(named, axis=0) - named
    slot_ids = jnp.arange(capacity, dtype=jnp.int32)[None, :, None]
    placer = (named.T[:, None, :] == 1) & (earlier.T[:, None, :] == slot_ids)
    token_gate = jnp.sum(
        jnp.where(onehot, gate_values[:, :, None], jnp.zeros((), jnp.float32)), axis=1
    )
    slot_gate = jnp.sum(placer.astype(jnp.float32) * token_gate.T[:, None, :], axis=2)
    return placer, slot_gate


def body(tokens, cotangent, routes, gate_values, gate_weight, up_weight, down_weight):
    tok_rows = tokens.shape[0]
    width = tokens.shape[1]
    top_count = routes.shape[1]
    experts = lax.axis_size("expert")
    groups = lax.axis_size("dp")
    quarter = width // groups
    capacity = min(tok_rows, max(2, 2 * tok_rows * top_count // experts))

    placer, _ = placement(routes, gate_values, experts, capacity)
    row_input = jnp.einsum(
        "est,td->esd", placer.astype(jnp.bfloat16), tokens, preferred_element_type=jnp.float32
    ).astype(jnp.bfloat16)
    arrived_input = lax.all_to_all(row_input, "expert", split_axis=0, concat_axis=0, tiled=True)
    inputs_all = lax.all_gather(
        arrived_input.reshape(experts * capacity, width), "dp", axis=0, tiled=True
    )

    col_routes = lax.all_gather(routes, "dp", axis=0, tiled=False)
    col_gates = lax.all_gather(gate_values, "dp", axis=0, tiled=False)
    col_cot = lax.all_gather(cotangent, "dp", axis=0, tiled=False)
    me = lax.axis_index("dp")
    cot_q = lax.dynamic_slice_in_dim(col_cot, me * quarter, quarter, axis=2)
    col_placer, col_slot_gate = jax.vmap(
        lambda r, g: placement(r, g, experts, capacity)
    )(col_routes, col_gates)
    picked_cot = jnp.einsum(
        "gest,gtd->egsd",
        col_placer.astype(jnp.bfloat16),
        cot_q,
        preferred_element_type=jnp.float32,
    )
    row_cot = (jnp.transpose(col_slot_gate, (1, 0, 2))[:, :, :, None] * picked_cot).astype(
        jnp.bfloat16
    )
    arrived_cot = lax.all_to_all(row_cot, "expert", split_axis=0, concat_axis=0, tiled=True)
    cot_quarter = jnp.transpose(arrived_cot, (1, 0, 2, 3)).reshape(
        groups * experts * capacity, quarter
    )

    gate_local = gate_weight[0]
    up_local = up_weight[0]
    down_local = down_weight[0]
    contract_last = (((1,), (1,)), ((), ()))
    gate_pre = lax.dot_general(
        gate_local, inputs_all, contract_last, preferred_element_type=jnp.float32
    )
    up_pre = lax.dot_general(
        up_local, inputs_all, contract_last, preferred_element_type=jnp.float32
    )
    hidden_part = (jax.nn.silu(gate_pre) * up_pre).astype(jnp.bfloat16)
    hidden_all = lax.all_gather(hidden_part, "dp", axis=0, tiled=True)
    contract_lead = (((0,), (0,)), ((), ()))
    expert_out = lax.dot_general(
        hidden_all, down_local, contract_lead, preferred_element_type=jnp.float32
    ).astype(jnp.bfloat16)
    grad_down = jnp.dot(hidden_all, cot_quarter, preferred_element_type=jnp.float32).astype(
        jnp.bfloat16
    )
    grad_hidden = lax.psum_scatter(
        lax.dot_general(down_local, cot_quarter, contract_last, preferred_element_type=jnp.float32),
        "dp",
        scatter_dimension=0,
        tiled=True,
    )
    sigma = jax.nn.sigmoid(gate_pre)
    grad_gate = (grad_hidden * up_pre * sigma * (1.0 + gate_pre * (1.0 - sigma))).astype(
        jnp.bfloat16
    )
    grad_up = (grad_hidden * jax.nn.silu(gate_pre)).astype(jnp.bfloat16)
    grad_gate_local = jnp.dot(grad_gate, inputs_all, preferred_element_type=jnp.float32).astype(
        jnp.bfloat16
    )
    grad_up_local = jnp.dot(grad_up, inputs_all, preferred_element_type=jnp.float32).astype(
        jnp.bfloat16
    )

    out_blocks = jnp.transpose(expert_out.reshape(groups, experts, capacity, quarter), (1, 0, 2, 3))
    returned = lax.all_to_all(out_blocks, "expert", split_axis=0, concat_axis=0, tiled=True)
    combine = col_placer.astype(jnp.float32) * col_slot_gate[:, :, :, None]
    mixed_q = jnp.einsum(
        "gest,egsd->gtd",
        combine,
        returned.astype(jnp.float32),
        precision=lax.Precision.HIGHEST,
        preferred_element_type=jnp.float32,
    ).astype(jnp.bfloat16)
    mixed = lax.all_to_all(mixed_q, "dp", split_axis=0, concat_axis=2, tiled=True)
    return (mixed[0], grad_gate_local[None], grad_up_local[None], grad_down[None])


def solution(mesh):
    in_specs = (
        P(("dp", "expert"), None),
        P(("dp", "expert"), None),
        P(("dp", "expert"), None),
        P(("dp", "expert"), None),
        P("expert", "dp", None),
        P("expert", "dp", None),
        P("expert", None, "dp"),
    )
    out_specs = (
        P(("dp", "expert"), None),
        P("expert", "dp", None),
        P("expert", "dp", None),
        P("expert", None, "dp"),
    )
    return jax.shard_map(body, mesh=mesh, in_specs=in_specs, out_specs=out_specs, check_vma=False)
```

time: 237 us -> 220 us (0.928)
  waiting for transfers between devices: 71.9 us -> 57.3 us
  blocking collectives: 88.2 us -> 80.6 us
  starting transfers between devices: 24.3 us -> 30.6 us
  local copies, waits for them, and re-layouts: 13.4 us -> 10.5 us
    all_to_all x2 -> x0, blocking collectives: 38.9 us -> none  [the longest x1 21.9 us: body(): lax.all_to_all(out_blocks, 'dp', split_axis=0, concat_axis=3, tiled=True)]
    all_gather x1, waiting for transfers between devices: 38.1 us -> 2.14 us  [body(): lax.all_gather(arrived_input.reshape(experts * capacity, width), 'dp', ax...]
    all_gather x0 -> x3, blocking collectives: none -> 31.3 us  [the longest x1 11.8 us: body(): col_cot = lax.all_gather(cotangent, 'dp', axis=0, tiled=False)]
    reduce_scatter x1, waiting for transfers between devices: 3.43 us -> 25.7 us  [body(): lax.psum_scatter(lax.dot_general(down_local, cot_quarter, contract_last,...]
    all_to_all x1, waiting for transfers between devices: 0.01 us -> 21.9 us  [body(): lax.all_to_all(row_cot, 'expert', split_axis=0, concat_axis=0, tiled=True)]
    all_to_all x1 -> x2, waiting for transfers between devices: 18.6 us -> 1.17 us  [the longest x1 1.17 us: body(): lax.all_to_all(mixed_q, 'dp', split_axis=0, concat_axis=2, tiled=True)]
    all_to_all x1, starting transfers between devices: 6.48 us -> 12.7 us  [body(): lax.all_to_all(row_cot, 'expert', split_axis=0, concat_axis=0, tiled=True)]
    all_gather x1, waiting for transfers between devices: 11.7 us -> 6.24 us  [body(): hidden_all = lax.all_gather(hidden_part, 'dp', axis=0, tiled=True)]
  transfers between devices with their start and end apart: 5 -> 6, of which waited for: 4 -> 5; matrix products, arithmetic and copies ran while one was open for 13% -> 14% of each run, Pallas kernels for 0% -> 0%
where the time goes in v1:
time: 220 us
  blocking collectives  80.6 us (37%)
  waiting for transfers between devices  57.3 us (26%)
  starting transfers between devices  30.6 us (14%)
  matrix products  26 us (12%)
  between operations  14 us (6%)
  local copies, waits for them, and re-layouts  10.5 us (5%)
    all_to_all x1, blocking collectives, body(): lax.all_to_all(row_input, 'expert', split_axis=0, concat_axis=0, tiled=True)  49.3 us
    reduce_scatter x1, waiting for transfers between devices, body(): lax.psum_scatter(lax.dot_general(down_local, cot_quarter, contract_last,...  25.7 us
    all_to_all x1, waiting for transfers between devices, body(): lax.all_to_all(row_cot, 'expert', split_axis=0, concat_axis=0, tiled=True)  21.9 us
    all_to_all x1, starting transfers between devices, body(): lax.all_to_all(out_blocks, 'expert', split_axis=0, concat_axis=0, tiled=T...  14.3 us
    all_to_all x1, starting transfers between devices, body(): lax.all_to_all(row_cot, 'expert', split_axis=0, concat_axis=0, tiled=True)  12.7 us
    all_gather x1, blocking collectives, body(): col_cot = lax.all_gather(cotangent, 'dp', axis=0, tiled=False)  11.8 us
    all_gather x1, blocking collectives, body(): col_gates = lax.all_gather(gate_values, 'dp', axis=0, tiled=False)  10 us
    all_gather x1, blocking collectives, body(): col_routes = lax.all_gather(routes, 'dp', axis=0, tiled=False)  9.52 us
  transfers between devices with their start and end apart: 6, of which 5 were waited for; matrix products, arithmetic and copies ran while one was open for 14% of the time, Pallas kernels for 0%

profile of v1, /device:TPU:1, one launch (start us, length us, event | category | flops | bytes accessed | tf_op | source)
XLA Modules:
  0.0 219.5 jit_solution(5703934371613074748)
XLA Ops:
  8.2 1.3 convolution_convert_fusion
  10.6 49.3 %all_to_all.30 = bf16[128,2,2048]{2,1,0:T(2,128)(2,1)S(1)} all-to-all(bf16[128,2,2048]{2,1,0:T(2,128)(2,1)S(1)} %copy.37), channel_id=1, replica_groups=mesh['dp'=4,'expert'=128] {'expert'}, dimensions={0} | all-to-all | bytes 2097152 | tf_op jit(solution)/shard_map/all_to_all | solution.py:33
  59.9 1.2 reshape.30
  61.1 9.5 %all-gather.3 = s32[4,16,8]{1,2,0:T(8,128)S(1)} all-gather(s32[1,16,8]{1,2,0:T(8,128)S(1)} %bitcast.81), channel_id=2, replica_groups=mesh['dp'=4,'expert'=128] {'dp'}, dimensions={0}, use_global_device_ids=true | all-gather | bytes 2560 | tf_op jit(solution)/shard_map/all_gather | solution.py:38
  71.0 10.0 %all-gather.4 = f32[4,16,8]{1,2,0:T(8,128)S(1)} all-gather(f32[1,16,8]{1,2,0:T(8,128)S(1)} %bitcast.82), channel_id=3, replica_groups=mesh['dp'=4,'expert'=128] {'dp'}, dimensions={0}, use_global_device_ids=true | all-gather | bytes 2560 | tf_op jit(solution)/shard_map/all_gather | solution.py:39
  81.0 11.8 %all-gather.2 = bf16[64,2048]{1,0:T(8,128)(2,1)S(1)} all-gather(bf16[16,2048]{1,0:T(8,128)(2,1)S(1)} %copy-done.1), channel_id=4, replica_groups=mesh['dp'=4,'expert'=128] {'dp'}, dimensions={0}, use_global_device_ids=true | all-gather | bytes 327680 | tf_op jit(solution)/shard_map/all_gather | solution.py:40
  93.6 2.1 copy.41
  95.7 12.7 %all-to-all-start.3 = ((bf16[128,4,2,512]{3,2,1,0:T(2,128)(2,1)}), bf16[128,4,2,512]{3,2,1,0:T(2,128)(2,1)S(1)}, u32[]{:S(2)}, u32[]{:S(2)}) async-start(bf16[128,4,2,512]{3,2,1,0:T(2,128)(2,1)} %copy.41), calls=%async_computation.3 | async-start | bytes 2097152 | tf_op jit(solution)/shard_map/all_to_all | solution.py:55
  108.5 2.1 all-gather.8.cloned.1.call-done
  110.7 3.9 %convolution_bitcast_fusion.2 = f32[192,1024]{1,0:T(8,128)S(1)} fusion(bf16[1024,2048]{1,0:T(8,128)(2,1)} %all-gather.8.cloned.1.call-done, bf16[1,192,2048]{2,1,0:T(8,128)(2,1)S(1)} %copy-done.6), kind=kOutput, calls=%fused_computation.12 | convolution fusion | flops 805306368 | bytes 5767168 | tf_op jit(solution)/shard_map/dot_general | solution.py:64
  114.6 2.6 %multiply_convert_fusion.2 = (bf16[192,1024]{1,0:T(8,128)(2,1)}, f32[192,1024]{1,0:T(8,128)}) fusion(f32[192,1024]{1,0:T(8,128)S(1)} %convolution_bitcast_fusion.2, bf16[1024,2048]{1,0:T(8,128)(2,1)S(1)} %copy-done.4, bf16[1,192,2048]{2,1,0:T(8,128)(2,1)S(1)} %copy-done.7), kind=kOutput, calls=%fused_computation.23 | convolution fusion | flops 806486016 | bytes 6946816 | tf_op jit(solution)/shard_map/dot_general | solution.py:67
  117.4 21.9 %all-to-all-done.3 = bf16[128,4,2,512]{3,2,1,0:T(2,128)(2,1)S(1)} async-done(((bf16[128,4,2,512]{3,2,1,0:T(2,128)(2,1)}), bf16[128,4,2,512]{3,2,1,0:T(2,128)(2,1)S(1)}, u32[]{:S(2)}, u32[]{:S(2)}) %all-to-all-start.3) | async-done | bytes 1048608 | tf_op jit(solution)/shard_map/all_to_all | solution.py:55
  140.5 2.7 %convolution_bitcast_fusion = f32[768,1024]{1,0:T(8,128)} fusion(bf16[1024,512]{1,0:T(8,128)(2,1)S(1)} %reshape.32, bf16[1,768,512]{2,1,0:T(8,128)(2,1)S(1)} %copy-done), kind=kOutput, calls=%fused_computation.7 | convolution fusion | flops 805306368 | bytes 4980736 | tf_op jit(solution)/shard_map/dot_general | solution.py:80
  143.3 6.2 %all-gather.10.cloned.1.call-done = bf16[768,1024]{1,0:T(8,128)(2,1)} async-done(((bf16[192,1024]{1,0:T(8,128)(2,1)}), bf16[768,1024]{1,0:T(8,128)(2,1)}) %all-gather.10.cloned.1.call-update) | async-done | bytes 1572880 | tf_op jit(solution)/shard_map/all_gather | solution.py:71
  149.5 3.4 %convolution_convert_fusion.3 = bf16[1024,512]{1,0:T(8,128)(2,1)} fusion(bf16[768,1024]{1,0:T(8,128)(2,1)} %all-gather.10.cloned.1.call-done, bf16[1,768,512]{2,1,0:T(8,128)(2,1)S(1)} %copy-done), kind=kOutput, calls=%fused_computation.8 | convolution fusion | flops 805830656 | bytes 3407872 | tf_op jit(solution)/shard_map/dot_general | solution.py:73
  152.9 1.5 reshape.31
  154.4 1.7 copy.51
  156.1 14.3 %all-to-all-start.1 = ((bf16[128,4,2,512]{3,2,1,0:T(2,128)(2,1)}), bf16[128,4,2,512]{3,2,1,0:T(2,128)(2,1)S(1)}, u32[]{:S(2)}, u32[]{:S(2)}) async-start(bf16[128,4,2,512]{3,2,1,0:T(2,128)(2,1)} %bitcast.74), calls=%async_computation.1 | async-start | bytes 2097152 | tf_op jit(solution)/shard_map/all_to_all | solution.py:98
  170.4 25.7 %reduce-scatter.2.cloned.1.call-done = f32[192,1024]{1,0:T(8,128)} async-done(((f32[768,1024]{1,0:T(8,128)}), f32[192,1024]{1,0:T(8,128)}) %reduce-scatter.2.cloned.1.call-update) | async-done | bytes 786448 | tf_op jit(solution)/shard_map/reduce_scatter | solution.py:79
  196.1 4.7 %fusion.1 = bf16[1,192,2048]{2,1,0:T(8,128)(2,1)} fusion(bf16[1024,2048]{1,0:T(8,128)(2,1)} %all-gather.8.cloned.1.call-done, f32[192,1024]{1,0:T(8,128)} %reduce-scatter.2.cloned.1.call-done, f32[192,1024]{1,0:T(8,128)} %copy-done.9), kind=kOutput, calls=%fused_computation.4 | convolution fusion | flops 806879232 | bytes 6553600 | tf_op jit(solution)/shard_map/dot_general | solution.py:93
  200.9 2.0 fusion
  202.9 1.6 fusion.4
  204.6 3.3 %all-to-all-start.2 = ((bf16[4,16,512]{2,1,0:T(8,128)(2,1)}), bf16[4,16,512]{2,1,0:T(8,128)(2,1)S(1)}, u32[]{:S(2)}, u32[]{:S(2)}) async-start(bf16[4,16,512]{2,1,0:T(8,128)(2,1)} %fusion.4), calls=%async_computation.2 | async-start | bytes 131072 | tf_op jit(solution)/shard_map/all_to_all | solution.py:107
  207.9 3.3 %fusion.3 = bf16[1,768,512]{2,1,0:T(8,128)(2,1)} fusion(bf16[768,1024]{1,0:T(8,128)(2,1)} %all-gather.10.cloned.1.call-done, bf16[1024,512]{1,0:T(8,128)(2,1)S(1)} %reshape.32), kind=kOutput, calls=%fused_computation.10 | convolution fusion | flops 805699584 | bytes 3407872 | tf_op jit(solution)/shard_map/dot_general | solution.py:76
  (51 shorter events, 6.6 us)
Async XLA Ops:
  7.2 133.4 %copy-start = (bf16[1,768,512]{2,1,0:T(8,128)(2,1)S(1)}, bf16[1,768,512]{2,1,0:T(8,128)(2,1)}, u32[]{:S(2)}) copy-start(bf16[1,768,512]{2,1,0:T(8,128)(2,1)} %param.13) | copy-start | bytes 2359300
  7.2 103.5 %all-gather.8.cloned.1.call-start = ((), (), s32[]{:S(2)}) async-start(), calls=%async_computation.5 | async-start | bytes 5242880 | tf_op jit(solution)/shard_map/all_gather | solution.py:34
  10.6 50.5 %copy-start.2 = (s32[16,8]{0,1:T(8,128)S(1)}, s32[16,8]{0,1:T(8,128)}, u32[]{:S(2)}) copy-start(s32[16,8]{0,1:T(8,128)} %param.9) | copy-start | bytes 1540
  10.6 60.3 %copy-start.3 = (f32[16,8]{0,1:T(8,128)S(1)}, f32[16,8]{0,1:T(8,128)}, u32[]{:S(2)}) copy-start(f32[16,8]{0,1:T(8,128)} %param.10) | copy-start | bytes 1540
  10.6 70.4 %copy-start.1 = (bf16[16,2048]{1,0:T(8,128)(2,1)S(1)}, bf16[16,2048]{1,0:T(8,128)(2,1)}, u32[]{:S(2)}) copy-start(bf16[16,2048]{1,0:T(8,128)(2,1)} %param.8) | copy-start | bytes 196612
  61.1 49.5 %copy-start.6 = (bf16[1,192,2048]{2,1,0:T(8,128)(2,1)S(1)}, bf16[1,192,2048]{2,1,0:T(8,128)(2,1)}, u32[]{:S(2)}) copy-start(bf16[1,192,2048]{2,1,0:T(8,128)(2,1)} %param.11) | copy-start | bytes 2359300
  95.7 43.6 %all-to-all-start.3 = ((bf16[128,4,2,512]{3,2,1,0:T(2,128)(2,1)}), bf16[128,4,2,512]{3,2,1,0:T(2,128)(2,1)S(1)}, u32[]{:S(2)}, u32[]{:S(2)}) async-start(bf16[128,4,2,512]{3,2,1,0:T(2,128)(2,1)} %copy.41), calls=%async_computation.3 | async-start | bytes 2097152 | tf_op jit(solution)/shard_map/all_to_all | solution.py:55
  108.4 6.1 %copy-start.7 = (bf16[1,192,2048]{2,1,0:T(8,128)(2,1)S(1)}, bf16[1,192,2048]{2,1,0:T(8,128)(2,1)}, u32[]{:S(2)}) copy-start(bf16[1,192,2048]{2,1,0:T(8,128)(2,1)} %param.12) | copy-start | bytes 2359300
  108.5 41.0 %all-gather.10.cloned.1.call-start = ((), (), s32[]{:S(2)}) async-start(), calls=%async_computation.6 | async-start | bytes 1966080 | tf_op jit(solution)/shard_map/all_gather | solution.py:71
  110.7 3.9 %copy-start.4 = (bf16[1024,2048]{1,0:T(8,128)(2,1)S(1)}, bf16[1024,2048]{1,0:T(8,128)(2,1)}, u32[]{:S(2)}) copy-start(bf16[1024,2048]{1,0:T(8,128)(2,1)} %all-gather.8.cloned.1.call-done) | copy-start | bytes 12582916
  114.5 2.6 %copy-start.9 = (f32[192,1024]{1,0:T(8,128)}, f32[192,1024]{1,0:T(8,128)S(1)}, u32[]{:S(2)}) copy-start(f32[192,1024]{1,0:T(8,128)S(1)} %convolution_bitcast_fusion.2) | copy-start | bytes 2359300
  117.2 79.0 %reduce-scatter.2.cloned.1.call-start = ((), (), s32[]{:S(2)}) async-start(), calls=%async_computation.7 | async-start | bytes 3932160 | tf_op jit(solution)/shard_map/reduce_scatter | solution.py:79
  156.1 46.8 %all-to-all-start.1 = ((bf16[128,4,2,512]{3,2,1,0:T(2,128)(2,1)}), bf16[128,4,2,512]{3,2,1,0:T(2,128)(2,1)S(1)}, u32[]{:S(2)}, u32[]{:S(2)}) async-start(bf16[128,4,2,512]{3,2,1,0:T(2,128)(2,1)} %bitcast.74), calls=%async_computation.1 | async-start | bytes 2097152 | tf_op jit(solution)/shard_map/all_to_all | solution.py:98
  196.1 4.7 %copy-start.5 = (bf16[1024,2048]{1,0:T(8,128)(2,1)S(1)}, bf16[1024,2048]{1,0:T(8,128)(2,1)}, u32[]{:S(2)}) copy-start(bf16[1024,2048]{1,0:T(8,128)(2,1)} %all-gather.8.cloned.1.call-done) | copy-start | bytes 12582916
  196.1 4.7 %copy-start.8 = (f32[192,1024]{1,0:T(8,128)S(1)}, f32[192,1024]{1,0:T(8,128)}, u32[]{:S(2)}) copy-start(f32[192,1024]{1,0:T(8,128)} %reduce-scatter.2.cloned.1.call-done) | copy-start | bytes 2359300
  196.1 4.7 %copy-start.10 = (f32[192,1024]{1,0:T(8,128)S(1)}, f32[192,1024]{1,0:T(8,128)}, u32[]{:S(2)}) copy-start(f32[192,1024]{1,0:T(8,128)} %copy-done.9) | copy-start | bytes 2359300
  196.1 4.7 %copy-start.11 = (f32[192,1024]{1,0:T(8,128)S(1)}, f32[192,1024]{1,0:T(8,128)}, u32[]{:S(2)}) copy-start(f32[192,1024]{1,0:T(8,128)} %get-tuple-element.5) | copy-start | bytes 2359300
  204.6 7.7 %all-to-all-start.2 = ((bf16[4,16,512]{2,1,0:T(8,128)(2,1)}), bf16[4,16,512]{2,1,0:T(8,128)(2,1)S(1)}, u32[]{:S(2)}, u32[]{:S(2)}) async-start(bf16[4,16,512]{2,1,0:T(8,128)(2,1)} %fusion.4), calls=%async_computation.2 | async-start | bytes 131072 | tf_op jit(solution)/shard_map/all_to_all | solution.py:107
Sparse Core Ops, SparseCore 0:
  61.2 49.3 all-gather.7
  117.3 32.1 all-gather.9
  152.3 43.7 reduce-scatter.1

commit v2 on v1

--- a/solution.py
+++ b/solution.py
@@ -35,11 +35,16 @@
         arrived_input.reshape(experts * capacity, width), "dp", axis=0, tiled=True
     )
 
-    col_routes = lax.all_gather(routes, "dp", axis=0, tiled=False)
-    col_gates = lax.all_gather(gate_values, "dp", axis=0, tiled=False)
-    col_cot = lax.all_gather(cotangent, "dp", axis=0, tiled=False)
+    packed = jnp.concatenate(
+        [cotangent.astype(jnp.float32), routes.astype(jnp.float32), gate_values], axis=1
+    )
+    col = lax.all_gather(packed, "dp", axis=0, tiled=False)
+    col_routes = col[:, :, width:width + top_count].astype(jnp.int32)
+    col_gates = col[:, :, width + top_count:]
     me = lax.axis_index("dp")
-    cot_q = lax.dynamic_slice_in_dim(col_cot, me * quarter, quarter, axis=2)
+    cot_q = lax.dynamic_slice_in_dim(col[:, :, :width], me * quarter, quarter, axis=2).astype(
+        jnp.bfloat16
+    )
     col_placer, col_slot_gate = jax.vmap(
         lambda r, g: placement(r, g, experts, capacity)
     )(col_routes, col_gates)
@@ -77,11 +82,13 @@
         jnp.bfloat16
     )
     grad_hidden = lax.psum_scatter(
-        lax.dot_general(down_local, cot_quarter, contract_last, preferred_element_type=jnp.float32),
+        lax.dot_general(
+            down_local, cot_quarter, contract_last, preferred_element_type=jnp.float32
+        ).astype(jnp.bfloat16),
         "dp",
         scatter_dimension=0,
         tiled=True,
-    )
+    ).astype(jnp.float32)
     sigma = jax.nn.sigmoid(gate_pre)
     grad_gate = (grad_hidden * up_pre * sigma * (1.0 + gate_pre * (1.0 - sigma))).astype(
         jnp.bfloat16

time: 220 us -> 216 us (0.982)
  waiting for transfers between devices: 57.3 us -> 78.3 us
  blocking collectives: 80.6 us -> 60.4 us
  starting transfers between devices: 30.6 us -> 26.5 us
    all_gather x1, waiting for transfers between devices: 6.24 us -> 28.7 us  [body(): hidden_all = lax.all_gather(hidden_part, 'dp', axis=0, tiled=True)]
    all_to_all x1, waiting for transfers between devices: 21.9 us -> 0.01 us  [body(): lax.all_to_all(row_cot, 'expert', split_axis=0, concat_axis=0, tiled=True)]
    all_gather x1, waiting for transfers between devices: 2.14 us -> 23.9 us  [body(): lax.all_gather(arrived_input.reshape(experts * capacity, width), 'dp', ax...]
    all_gather x3 -> x1, blocking collectives: 31.3 us -> 11.2 us  [body(): col = lax.all_gather(packed, 'dp', axis=0, tiled=False)]
    reduce_scatter x1, waiting for transfers between devices: 25.7 us -> 14.1 us  [body(): lax.psum_scatter(lax.dot_general(down_local, cot_quarter, contract_last,...]
    all_to_all x1, waiting for transfers between devices: 0.01 us -> 10.4 us  [body(): lax.all_to_all(out_blocks, 'expert', split_axis=0, concat_axis=0, tiled=T...]
    all_to_all x1, starting transfers between devices: 12.7 us -> 8.65 us  [body(): lax.all_to_all(row_cot, 'expert', split_axis=0, concat_axis=0, tiled=True)]
  transfers between devices with their start and end apart: 6 -> 6, of which waited for: 5 -> 5; matrix products, arithmetic and copies ran while one was open for 14% -> 13% of each run, Pallas kernels for 0% -> 0%
where the time goes in v2:
time: 216 us; the launch traced here: 215 us
  waiting for transfers between devices  78.3 us (36%)
  blocking collectives  60.4 us (28%)
  starting transfers between devices  26.5 us (12%)
  matrix products  25.7 us (12%)
  between operations  14 us (6%)
  local copies, waits for them, and re-layouts  9.6 us (4%)
    all_to_all x1, blocking collectives, body(): lax.all_to_all(row_input, 'expert', split_axis=0, concat_axis=0, tiled=True)  49.1 us
    all_gather x1, waiting for transfers between devices, body(): hidden_all = lax.all_gather(hidden_part, 'dp', axis=0, tiled=True)  28.7 us
    all_gather x1, waiting for transfers between devices, body(): lax.all_gather(arrived_input.reshape(experts * capacity, width), 'dp', ax...  23.9 us
    all_to_all x1, starting transfers between devices, body(): lax.all_to_all(out_blocks, 'expert', split_axis=0, concat_axis=0, tiled=T...  14.3 us
    reduce_scatter x1, waiting for transfers between devices, body(): lax.psum_scatter(lax.dot_general(down_local, cot_quarter, contract_last,...  14.1 us
    all_gather x1, blocking collectives, body(): col = lax.all_gather(packed, 'dp', axis=0, tiled=False)  11.2 us
    all_to_all x1, waiting for transfers between devices, body(): lax.all_to_all(out_blocks, 'expert', split_axis=0, concat_axis=0, tiled=T...  10.4 us
    all_to_all x1, starting transfers between devices, body(): lax.all_to_all(row_cot, 'expert', split_axis=0, concat_axis=0, tiled=True)  8.65 us
  transfers between devices with their start and end apart: 6, of which 5 were waited for; matrix products, arithmetic and copies ran while one was open for 13% of the time, Pallas kernels for 0%

profile of v2, /device:TPU:1, one launch (start us, length us, event | category | flops | bytes accessed | tf_op | source)
XLA Modules:
  0.0 215.2 jit_solution(4041124225692408910)
XLA Ops:
  7.2 0.8 copy.36
  8.2 1.3 convolution_convert_fusion
  9.5 1.1 copy.37
  10.6 49.1 %all_to_all.30 = bf16[128,2,2048]{2,1,0:T(2,128)(2,1)S(1)} all-to-all(bf16[128,2,2048]{2,1,0:T(2,128)(2,1)S(1)} %copy.37), channel_id=1, replica_groups=mesh['dp'=4,'expert'=128] {'expert'}, dimensions={0} | all-to-all | bytes 2097152 | tf_op jit(solution)/shard_map/all_to_all | solution.py:33
  59.7 1.2 reshape.30
  61.2 11.2 %all-gather = f32[64,2064]{1,0:T(8,128)S(1)} all-gather(f32[16,2064]{1,0:T(8,128)S(1)} %concatenate.3), channel_id=2, replica_groups=mesh['dp'=4,'expert'=128] {'dp'}, dimensions={0}, use_global_device_ids=true | all-gather | bytes 660480 | tf_op jit(solution)/shard_map/all_gather | solution.py:41
  73.6 2.1 copy.41
  75.6 8.7 %all-to-all-start.3 = ((bf16[128,4,2,512]{3,2,1,0:T(2,128)(2,1)}), bf16[128,4,2,512]{3,2,1,0:T(2,128)(2,1)S(1)}, u32[]{:S(2)}, u32[]{:S(2)}) async-start(bf16[128,4,2,512]{3,2,1,0:T(2,128)(2,1)} %copy.41), calls=%async_computation.3 | async-start | bytes 2097152 | tf_op jit(solution)/shard_map/all_to_all | solution.py:60
  84.4 23.9 %all-gather.4.cloned.1.call-done = bf16[1024,2048]{1,0:T(8,128)(2,1)} async-done(((bf16[256,2048]{1,0:T(8,128)(2,1)}), bf16[1024,2048]{1,0:T(8,128)(2,1)}) %all-gather.4.cloned.1.call-update) | async-done | bytes 4194320 | tf_op jit(solution)/shard_map/all_gather | solution.py:34
  108.3 3.9 %convolution_bitcast_fusion.1 = f32[192,1024]{1,0:T(8,128)S(1)} fusion(bf16[1024,2048]{1,0:T(8,128)(2,1)} %all-gather.4.cloned.1.call-done, bf16[1,192,2048]{2,1,0:T(8,128)(2,1)S(1)} %copy-done.8), kind=kOutput, calls=%fused_computation.13 | convolution fusion | flops 805306368 | bytes 5767168 | tf_op jit(solution)/shard_map/dot_general | solution.py:69
  112.2 4.1 %multiply_convert_fusion = (bf16[192,1024]{1,0:T(8,128)(2,1)}, f32[192,1024]{1,0:T(8,128)}) fusion(f32[192,1024]{1,0:T(8,128)S(1)} %convolution_bitcast_fusion.1, bf16[1024,2048]{1,0:T(8,128)(2,1)S(1)} %copy-done.6, bf16[1,192,2048]{2,1,0:T(8,128)(2,1)} %param.12), kind=kOutput, calls=%fused_computation.28 | convolution fusion | flops 806486016 | bytes 6946816 | tf_op jit(solution)/shard_map/dot_general | solution.py:72
  117.7 2.2 %fusion.3 = bf16[768,1024]{1,0:T(8,128)(2,1)} fusion(bf16[1024,512]{1,0:T(8,128)(2,1)S(1)} %reshape.32, bf16[1,768,512]{2,1,0:T(8,128)(2,1)S(1)} %copy-done), kind=kOutput, calls=%fused_computation.9 | convolution fusion | flops 806092800 | bytes 3407872 | tf_op jit(solution)/shard_map/dot_general | solution.py:85
  119.9 28.7 %all-gather.6.cloned.1.call-done = bf16[768,1024]{1,0:T(8,128)(2,1)} async-done(((bf16[192,1024]{1,0:T(8,128)(2,1)}), bf16[768,1024]{1,0:T(8,128)(2,1)}) %all-gather.6.cloned.1.call-update) | async-done | bytes 1572880 | tf_op jit(solution)/shard_map/all_gather | solution.py:76
  148.7 2.4 %convolution_convert_fusion.4 = bf16[1024,512]{1,0:T(8,128)(2,1)S(1)} fusion(bf16[768,1024]{1,0:T(8,128)(2,1)} %all-gather.6.cloned.1.call-done, bf16[1,768,512]{2,1,0:T(8,128)(2,1)S(1)} %copy-done), kind=kOutput, calls=%fused_computation.8 | convolution fusion | flops 805830656 | bytes 3407872 | tf_op jit(solution)/shard_map/dot_general | solution.py:78
  151.6 1.8 copy.51
  153.3 14.3 %all-to-all-start.1 = ((bf16[128,4,2,512]{3,2,1,0:T(2,128)(2,1)}), bf16[128,4,2,512]{3,2,1,0:T(2,128)(2,1)S(1)}, u32[]{:S(2)}, u32[]{:S(2)}) async-start(bf16[128,4,2,512]{3,2,1,0:T(2,128)(2,1)} %bitcast.70), calls=%async_computation.1 | async-start | bytes 2097152 | tf_op jit(solution)/shard_map/all_to_all | solution.py:105
  167.6 14.1 %reduce-scatter.2.cloned.1.call-done = bf16[192,1024]{1,0:T(8,128)(2,1)} async-done(((bf16[768,1024]{1,0:T(8,128)(2,1)}), bf16[192,1024]{1,0:T(8,128)(2,1)}) %reduce-scatter.2.cloned.1.call-update) | async-done | bytes 393232 | tf_op jit(solution)/shard_map/reduce_scatter | solution.py:84
  181.7 4.4 %fusion.1 = bf16[1,192,2048]{2,1,0:T(8,128)(2,1)} fusion(bf16[1024,2048]{1,0:T(8,128)(2,1)} %all-gather.4.cloned.1.call-done, bf16[192,1024]{1,0:T(8,128)(2,1)} %reduce-scatter.2.cloned.1.call-done, f32[192,1024]{1,0:T(8,128)S(1)} %copy-done.11), kind=kOutput, calls=%fused_computation.4 | convolution fusion | flops 807075840 | bytes 6160384 | tf_op jit(solution)/shard_map/dot_general | solution.py:100
  186.1 2.0 fusion
  188.2 10.4 %all-to-all-done.1 = bf16[128,4,2,512]{3,2,1,0:T(2,128)(2,1)S(1)} async-done(((bf16[128,4,2,512]{3,2,1,0:T(2,128)(2,1)}), bf16[128,4,2,512]{3,2,1,0:T(2,128)(2,1)S(1)}, u32[]{:S(2)}, u32[]{:S(2)}) %all-to-all-start.1) | async-done | bytes 1048608 | tf_op jit(solution)/shard_map/all_to_all | solution.py:105
  198.5 1.6 fusion.5
  200.2 3.3 %all-to-all-start.2 = ((bf16[4,16,512]{2,1,0:T(8,128)(2,1)}), bf16[4,16,512]{2,1,0:T(8,128)(2,1)S(1)}, u32[]{:S(2)}, u32[]{:S(2)}) async-start(bf16[4,16,512]{2,1,0:T(8,128)(2,1)} %fusion.5), calls=%async_computation.2 | async-start | bytes 131072 | tf_op jit(solution)/shard_map/all_to_all | solution.py:114
  203.5 3.3 %fusion.4 = bf16[1,768,512]{2,1,0:T(8,128)(2,1)} fusion(bf16[768,1024]{1,0:T(8,128)(2,1)} %all-gather.6.cloned.1.call-done, bf16[1024,512]{1,0:T(8,128)(2,1)S(1)} %copy-done.2), kind=kOutput, calls=%fused_computation.11 | convolution fusion | flops 805699584 | bytes 3407872 | tf_op jit(solution)/shard_map/dot_general | solution.py:81
  206.8 1.2 all-to-all-done.2
  (57 shorter events, 4.1 us)
Async XLA Ops:
  7.2 110.5 %copy-start = (bf16[1,768,512]{2,1,0:T(8,128)(2,1)S(1)}, bf16[1,768,512]{2,1,0:T(8,128)(2,1)}, u32[]{:S(2)}) copy-start(bf16[1,768,512]{2,1,0:T(8,128)(2,1)} %param.13) | copy-start | bytes 2359300
  7.2 101.1 %all-gather.4.cloned.1.call-start = ((), (), s32[]{:S(2)}) async-start(), calls=%async_computation.5 | async-start | bytes 5242880 | tf_op jit(solution)/shard_map/all_gather | solution.py:34
  59.7 1.3 copy-start.4
  59.7 1.3 copy-start.5
  59.7 1.4 copy-start.3
  73.6 34.7 %copy-start.8 = (bf16[1,192,2048]{2,1,0:T(8,128)(2,1)S(1)}, bf16[1,192,2048]{2,1,0:T(8,128)(2,1)}, u32[]{:S(2)}) copy-start(bf16[1,192,2048]{2,1,0:T(8,128)(2,1)} %param.11) | copy-start | bytes 2359300
  75.6 40.9 %all-to-all-start.3 = ((bf16[128,4,2,512]{3,2,1,0:T(2,128)(2,1)}), bf16[128,4,2,512]{3,2,1,0:T(2,128)(2,1)S(1)}, u32[]{:S(2)}, u32[]{:S(2)}) async-start(bf16[128,4,2,512]{3,2,1,0:T(2,128)(2,1)} %copy.41), calls=%async_computation.3 | async-start | bytes 2097152 | tf_op jit(solution)/shard_map/all_to_all | solution.py:60
  84.3 64.4 %all-gather.6.cloned.1.call-start = ((), (), s32[]{:S(2)}) async-start(), calls=%async_computation.6 | async-start | bytes 1966080 | tf_op jit(solution)/shard_map/all_gather | solution.py:76
  108.3 3.9 %copy-start.6 = (bf16[1024,2048]{1,0:T(8,128)(2,1)S(1)}, bf16[1024,2048]{1,0:T(8,128)(2,1)}, u32[]{:S(2)}) copy-start(bf16[1024,2048]{1,0:T(8,128)(2,1)} %all-gather.4.cloned.1.call-done) | copy-start | bytes 12582916
  112.2 4.1 %copy-start.10 = (f32[192,1024]{1,0:T(8,128)}, f32[192,1024]{1,0:T(8,128)S(1)}, u32[]{:S(2)}) copy-start(f32[192,1024]{1,0:T(8,128)S(1)} %convolution_bitcast_fusion.1) | copy-start | bytes 2359300
  116.3 65.4 %reduce-scatter.2.cloned.1.call-start = ((), (), s32[]{:S(2)}) async-start(), calls=%async_computation.7 | async-start | bytes 1966080 | tf_op jit(solution)/shard_map/reduce_scatter | solution.py:84
  117.7 2.2 %copy-start.1 = (bf16[1024,512]{1,0:T(8,128)(2,1)}, bf16[1024,512]{1,0:T(8,128)(2,1)S(1)}, u32[]{:S(2)}) copy-start(bf16[1024,512]{1,0:T(8,128)(2,1)S(1)} %reshape.32) | copy-start | bytes 3145732
  151.5 30.2 %copy-start.11 = (f32[192,1024]{1,0:T(8,128)S(1)}, f32[192,1024]{1,0:T(8,128)}, u32[]{:S(2)}) copy-start(f32[192,1024]{1,0:T(8,128)} %copy-done.10) | copy-start | bytes 2359300
  153.3 45.2 %all-to-all-start.1 = ((bf16[128,4,2,512]{3,2,1,0:T(2,128)(2,1)}), bf16[128,4,2,512]{3,2,1,0:T(2,128)(2,1)S(1)}, u32[]{:S(2)}, u32[]{:S(2)}) async-start(bf16[128,4,2,512]{3,2,1,0:T(2,128)(2,1)} %bitcast.70), calls=%async_computation.1 | async-start | bytes 2097152 | tf_op jit(solution)/shard_map/all_to_all | solution.py:105
  181.7 4.4 %copy-start.7 = (bf16[1024,2048]{1,0:T(8,128)(2,1)S(1)}, bf16[1024,2048]{1,0:T(8,128)(2,1)}, u32[]{:S(2)}) copy-start(bf16[1024,2048]{1,0:T(8,128)(2,1)} %all-gather.4.cloned.1.call-done) | copy-start | bytes 12582916
  181.7 4.4 %copy-start.9 = (bf16[192,1024]{1,0:T(8,128)(2,1)S(1)}, bf16[192,1024]{1,0:T(8,128)(2,1)}, u32[]{:S(2)}) copy-start(bf16[192,1024]{1,0:T(8,128)(2,1)} %reduce-scatter.2.cloned.1.call-done) | copy-start | bytes 1179652
  181.7 4.4 %copy-start.12 = (f32[192,1024]{1,0:T(8,128)S(1)}, f32[192,1024]{1,0:T(8,128)}, u32[]{:S(2)}) copy-start(f32[192,1024]{1,0:T(8,128)} %copy-done.10) | copy-start | bytes 2359300
  181.7 4.4 %copy-start.13 = (f32[192,1024]{1,0:T(8,128)S(1)}, f32[192,1024]{1,0:T(8,128)}, u32[]{:S(2)}) copy-start(f32[192,1024]{1,0:T(8,128)} %get-tuple-element.7) | copy-start | bytes 2359300
  186.1 17.3 %copy-start.2 = (bf16[1024,512]{1,0:T(8,128)(2,1)S(1)}, bf16[1024,512]{1,0:T(8,128)(2,1)}, u32[]{:S(2)}) copy-start(bf16[1024,512]{1,0:T(8,128)(2,1)} %copy-done.1) | copy-start | bytes 3145732
  200.2 7.7 %all-to-all-start.2 = ((bf16[4,16,512]{2,1,0:T(8,128)(2,1)}), bf16[4,16,512]{2,1,0:T(8,128)(2,1)S(1)}, u32[]{:S(2)}, u32[]{:S(2)}) async-start(bf16[4,16,512]{2,1,0:T(8,128)(2,1)} %fusion.5), calls=%async_computation.2 | async-start | bytes 131072 | tf_op jit(solution)/shard_map/all_to_all | solution.py:114
Sparse Core Ops, SparseCore 0:
  61.1 47.1 all-gather.3
  116.4 32.2 all-gather.5
  151.5 30.1 reduce-scatter.1

commit v3 on v2

--- a/solution.py
+++ b/solution.py
@@ -30,10 +30,13 @@
     row_input = jnp.einsum(
         "est,td->esd", placer.astype(jnp.bfloat16), tokens, preferred_element_type=jnp.float32
     ).astype(jnp.bfloat16)
-    arrived_input = lax.all_to_all(row_input, "expert", split_axis=0, concat_axis=0, tiled=True)
-    inputs_all = lax.all_gather(
-        arrived_input.reshape(experts * capacity, width), "dp", axis=0, tiled=True
-    )
+    inputs_by_slot = []
+    for slot in range(capacity):
+        arrived_input = lax.all_to_all(
+            row_input[:, slot], "expert", split_axis=0, concat_axis=0, tiled=True
+        )
+        inputs_by_slot.append(lax.all_gather(arrived_input, "dp", axis=0, tiled=True))
+    inputs_all = jnp.concatenate(inputs_by_slot, axis=0)
 
     packed = jnp.concatenate(
         [cotangent.astype(jnp.float32), routes.astype(jnp.float32), gate_values], axis=1
@@ -58,7 +61,7 @@
         jnp.bfloat16
     )
     arrived_cot = lax.all_to_all(row_cot, "expert", split_axis=0, concat_axis=0, tiled=True)
-    cot_quarter = jnp.transpose(arrived_cot, (1, 0, 2, 3)).reshape(
+    cot_quarter = jnp.transpose(arrived_cot, (2, 1, 0, 3)).reshape(
         groups * experts * capacity, quarter
     )
 
@@ -82,13 +85,11 @@
         jnp.bfloat16
     )
     grad_hidden = lax.psum_scatter(
-        lax.dot_general(
-            down_local, cot_quarter, contract_last, preferred_element_type=jnp.float32
-        ).astype(jnp.bfloat16),
+        lax.dot_general(down_local, cot_quarter, contract_last, preferred_element_type=jnp.float32),
         "dp",
         scatter_dimension=0,
         tiled=True,
-    ).astype(jnp.float32)
+    )
     sigma = jax.nn.sigmoid(gate_pre)
     grad_gate = (grad_hidden * up_pre * sigma * (1.0 + gate_pre * (1.0 - sigma))).astype(
         jnp.bfloat16
@@ -101,7 +102,7 @@
         jnp.bfloat16
     )
 
-    out_blocks = jnp.transpose(expert_out.reshape(groups, experts, capacity, quarter), (1, 0, 2, 3))
+    out_blocks = jnp.transpose(expert_out.reshape(capacity, groups, experts, quarter), (2, 1, 0, 3))
     returned = lax.all_to_all(out_blocks, "expert", split_axis=0, concat_axis=0, tiled=True)
     combine = col_placer.astype(jnp.float32) * col_slot_gate[:, :, :, None]
     mixed_q = jnp.einsum(

time: 216 us -> 230 us (1.065)
  blocking collectives: 60.4 us -> 76.2 us
  waiting for transfers between devices: 78.3 us -> 70.7 us
    all_to_all x1 -> x2, blocking collectives: 49.1 us -> 64.6 us  [body(): lax.all_to_all(row_input[:, slot], 'expert', split_axis=0, concat_axis=0,...]
    all_to_all x1, waiting for transfers between devices: 10.4 us -> 0.01 us  [body(): lax.all_to_all(out_blocks, 'expert', split_axis=0, concat_axis=0, tiled=T...]
    reduce_scatter x1, waiting for transfers between devices: 14.1 us -> 24.4 us  [body(): lax.psum_scatter(lax.dot_general(down_local, cot_quarter, contract_last,...]
    all_to_all x1, waiting for transfers between devices: 0.01 us -> 6.84 us  [body(): lax.all_to_all(row_cot, 'expert', split_axis=0, concat_axis=0, tiled=True)]
    all_gather x1 -> x2, waiting for transfers between devices: 23.9 us -> 17.2 us  [body(): lax.all_gather(arrived_input, 'dp', axis=0, tiled=True)]
    all_gather x1, waiting for transfers between devices: 28.7 us -> 22.2 us  [body(): hidden_all = lax.all_gather(hidden_part, 'dp', axis=0, tiled=True)]
    dot_general x1, matrix products: 2.04 us -> 5 us  [body(): jnp.dot(grad_gate, inputs_all, preferred_element_type=jnp.float32)]
    all_to_all x0 -> x3, local copies, waits for them, and re-layouts: none -> 2.5 us  [the longest x2 2.19 us: body(): lax.all_to_all(row_input[:, slot], 'expert', split_axis=0, concat_axis=0,...]
  transfers between devices with their start and end apart: 6 -> 7, of which waited for: 5 -> 4; matrix products, arithmetic and copies ran while one was open for 13% -> 14% of each run, Pallas kernels for 0% -> 0%
where the time goes in v3:
time: 230 us; the launch traced here: 229 us
  blocking collectives  76.2 us (33%)
  waiting for transfers between devices  70.7 us (31%)
  matrix products  27.7 us (12%)
  starting transfers between devices  26.8 us (12%)
  between operations  14 us (6%)
  local copies, waits for them, and re-layouts  10.7 us (5%)
  other arithmetic  2.66 us (1%)
    all_to_all x2, blocking collectives, body(): lax.all_to_all(row_input[:, slot], 'expert', split_axis=0, concat_axis=0,...  64.6 us
    reduce_scatter x1, waiting for transfers between devices, body(): lax.psum_scatter(lax.dot_general(down_local, cot_quarter, contract_last,...  24.4 us
    all_gather x1, waiting for transfers between devices, body(): hidden_all = lax.all_gather(hidden_part, 'dp', axis=0, tiled=True)  22.2 us
    all_gather x2, waiting for transfers between devices, body(): lax.all_gather(arrived_input, 'dp', axis=0, tiled=True)  17.2 us
    all_to_all x1, starting transfers between devices, body(): lax.all_to_all(out_blocks, 'expert', split_axis=0, concat_axis=0, tiled=T...  14.3 us
    all_gather x1, blocking collectives, body(): col = lax.all_gather(packed, 'dp', axis=0, tiled=False)  11.6 us
    all_to_all x1, starting transfers between devices, body(): lax.all_to_all(row_cot, 'expert', split_axis=0, concat_axis=0, tiled=True)  8.91 us
    all_to_all x1, waiting for transfers between devices, body(): lax.all_to_all(row_cot, 'expert', split_axis=0, concat_axis=0, tiled=True)  6.84 us
  transfers between devices with their start and end apart: 7, of which 4 were waited for; matrix products, arithmetic and copies ran while one was open for 14% of the time, Pallas kernels for 0%

profile of v3, /device:TPU:1, one launch (start us, length us, event | category | flops | bytes accessed | tf_op | source)
XLA Modules:
  0.0 228.8 jit_solution(16926733251695322274)
XLA Ops:
  8.2 1.3 convolution_convert_fusion
  11.5 38.8 %all_to_all.43 = bf16[128,2,1024]{2,1,0:T(2,128)(2,1)S(1)} all-to-all(bf16[128,2,1024]{2,1,0:T(2,128)(2,1)S(1)} %reshape.41), channel_id=1, replica_groups=mesh['dp'=4,'expert'=128] {'expert'}, dimensions={0} | all-to-all | bytes 1048576 | tf_op jit(solution)/shard_map/all_to_all | solution.py:35
  50.8 1.1 copy.54
  51.9 1.0 reduce.1
  53.3 25.8 %all_to_all.44 = bf16[128,2,1024]{2,1,0:T(2,128)(2,1)S(1)} all-to-all(bf16[128,2,1024]{2,1,0:T(2,128)(2,1)S(1)} %reshape.43), channel_id=1, replica_groups=mesh['dp'=4,'expert'=128] {'expert'}, dimensions={0} | all-to-all | bytes 1048576 | tf_op jit(solution)/shard_map/all_to_all | solution.py:35
  79.5 1.1 copy.52
  80.9 11.6 %all-gather = f32[64,2064]{1,0:T(8,128)S(1)} all-gather(f32[16,2064]{1,0:T(8,128)S(1)} %concatenate.6), channel_id=2, replica_groups=mesh['dp'=4,'expert'=128] {'dp'}, dimensions={0}, use_global_device_ids=true | all-gather | bytes 660480 | tf_op jit(solution)/shard_map/all_gather | solution.py:44
  93.6 2.0 copy.58
  95.7 8.9 %all-to-all-start.4 = ((bf16[128,4,2,512]{3,2,1,0:T(2,128)(2,1)}), bf16[128,4,2,512]{3,2,1,0:T(2,128)(2,1)S(1)}, u32[]{:S(2)}, u32[]{:S(2)}) async-start(bf16[128,4,2,512]{3,2,1,0:T(2,128)(2,1)} %copy.58), calls=%async_computation.4 | async-start | bytes 2097152 | tf_op jit(solution)/shard_map/all_to_all | solution.py:63
  104.9 17.2 %all-gather.9.cloned.1.call-done = bf16[512,1,2048]{2,0,1:T(8,128)(2,1)} async-done(((bf16[128,1,2048]{2,0,1:T(8,128)(2,1)}), bf16[512,1,2048]{2,0,1:T(8,128)(2,1)}) %all-gather.9.cloned.1.call-update) | async-done | bytes 2097168 | tf_op jit(solution)/shard_map/all_gather | solution.py:38
  122.1 3.9 %convolution_bitcast_fusion.2 = f32[192,1024]{1,0:T(8,128)S(1)} fusion(bf16[1,192,2048]{2,1,0:T(8,128)(2,1)S(1)} %copy-done.6, bf16[512,2048]{1,0:T(8,128)(2,1)} %bitcast.83, bf16[512,2048]{1,0:T(8,128)(2,1)} %bitcast.87), kind=kOutput, calls=%fused_computation.13 | convolution fusion | flops 813694976 | bytes 5767168 | tf_op jit(solution)/shard_map/dot_general | solution.py:72
  126.0 2.6 %multiply_convert_fusion.2 = (bf16[192,1024]{1,0:T(8,128)(2,1)}, f32[192,1024]{1,0:T(8,128)}) fusion(f32[192,1024]{1,0:T(8,128)S(1)} %convolution_bitcast_fusion.2, bf16[1,192,2048]{2,1,0:T(8,128)(2,1)S(1)} %copy-done.7, bf16[512,2048]{1,0:T(8,128)(2,1)S(1)} %bitcast.86, bf16[512,2048]{1,0:T(8,128)(2,1)S(1)} %bitcast.90), kind=kOutput, calls=%fused_computation.24 | convolution fusion | flops 814874624 | bytes 6946816 | tf_op jit(solution)/shard_map/dot_general | solution.py:75
  128.7 6.8 %all-to-all-done.4 = bf16[128,4,2,512]{3,2,1,0:T(2,128)(2,1)S(1)} async-done(((bf16[128,4,2,512]{3,2,1,0:T(2,128)(2,1)}), bf16[128,4,2,512]{3,2,1,0:T(2,128)(2,1)S(1)}, u32[]{:S(2)}, u32[]{:S(2)}) %all-to-all-start.4) | async-done | bytes 1048608 | tf_op jit(solution)/shard_map/all_to_all | solution.py:63
  135.8 2.7 %convolution_bitcast_fusion = f32[768,1024]{1,0:T(8,128)} fusion(bf16[1024,512]{1,0:T(8,128)(2,1)S(1)} %bitcast.72, bf16[1,768,512]{2,1,0:T(8,128)(2,1)S(1)} %copy-done), kind=kOutput, calls=%fused_computation.8 | convolution fusion | flops 805306368 | bytes 4980736 | tf_op jit(solution)/shard_map/dot_general | solution.py:88
  138.5 22.2 %all-gather.7.cloned.1.call-done = bf16[768,1024]{1,0:T(8,128)(2,1)} async-done(((bf16[192,1024]{1,0:T(8,128)(2,1)}), bf16[768,1024]{1,0:T(8,128)(2,1)}) %all-gather.7.cloned.1.call-update) | async-done | bytes 1572880 | tf_op jit(solution)/shard_map/all_gather | solution.py:79
  160.7 2.4 %convolution_convert_fusion.3 = bf16[1024,512]{1,0:T(8,128)(2,1)S(1)} fusion(bf16[768,1024]{1,0:T(8,128)(2,1)} %all-gather.7.cloned.1.call-done, bf16[1,768,512]{2,1,0:T(8,128)(2,1)S(1)} %copy-done), kind=kOutput, calls=%fused_computation.9 | convolution fusion | flops 805830656 | bytes 3407872 | tf_op jit(solution)/shard_map/dot_general | solution.py:81
  163.1 2.1 copy.68
  165.2 14.3 %all-to-all-start.2 = ((bf16[128,4,2,512]{3,2,1,0:T(2,128)(2,1)}), bf16[128,4,2,512]{3,2,1,0:T(2,128)(2,1)S(1)}, u32[]{:S(2)}, u32[]{:S(2)}) async-start(bf16[128,4,2,512]{3,2,1,0:T(2,128)(2,1)} %bitcast.74), calls=%async_computation.2 | async-start | bytes 2097152 | tf_op jit(solution)/shard_map/all_to_all | solution.py:106
  179.5 3.3 %fusion.3 = bf16[1,768,512]{2,1,0:T(8,128)(2,1)} fusion(bf16[768,1024]{1,0:T(8,128)(2,1)} %all-gather.7.cloned.1.call-done, bf16[1024,512]{1,0:T(8,128)(2,1)S(1)} %bitcast.73), kind=kOutput, calls=%fused_computation.11 | convolution fusion | flops 805699584 | bytes 3407872 | tf_op jit(solution)/shard_map/dot_general | solution.py:84
  182.8 24.4 %reduce-scatter.2.cloned.1.call-done = f32[192,1024]{1,0:T(8,128)} async-done(((f32[768,1024]{1,0:T(8,128)}), f32[192,1024]{1,0:T(8,128)}) %reduce-scatter.2.cloned.1.call-update) | async-done | bytes 786448 | tf_op jit(solution)/shard_map/reduce_scatter | solution.py:87
  207.2 5.0 %fusion = bf16[1,192,2048]{2,1,0:T(8,128)(2,1)} fusion(f32[192,1024]{1,0:T(8,128)} %copy-done.9, f32[192,1024]{1,0:T(8,128)} %reduce-scatter.2.cloned.1.call-done, f32[192,1024]{1,0:T(8,128)} %get-tuple-element.9, bf16[512,2048]{1,0:T(8,128)(2,1)} %bitcast.84, bf16[512,2048]{1,0:T(8,128)(2,1)} %bitcast.88), kind=kOutput, calls=%fused_computation.4 | convolution fusion | flops 816054272 | bytes 7340032 | tf_op jit(solution)/shard_map/dot_general | solution.py:98
  212.2 1.6 fusion.4
  213.8 3.3 %all-to-all-start.3 = ((bf16[4,16,512]{2,1,0:T(8,128)(2,1)}), bf16[4,16,512]{2,1,0:T(8,128)(2,1)S(1)}, u32[]{:S(2)}, u32[]{:S(2)}) async-start(bf16[4,16,512]{2,1,0:T(8,128)(2,1)} %fusion.4), calls=%async_computation.3 | async-start | bytes 131072 | tf_op jit(solution)/shard_map/all_to_all | solution.py:115
  217.2 4.4 %fusion.1 = bf16[1,192,2048]{2,1,0:T(8,128)(2,1)} fusion(f32[192,1024]{1,0:T(8,128)S(1)} %copy-done.8, f32[192,1024]{1,0:T(8,128)} %copy-done.9, bf16[512,2048]{1,0:T(8,128)(2,1)} %bitcast.85, bf16[512,2048]{1,0:T(8,128)(2,1)} %bitcast.89), kind=kOutput, calls=%fused_computation.5 | convolution fusion | flops 815267840 | bytes 6553600 | tf_op jit(solution)/shard_map/dot_general | solution.py:101
  (59 shorter events, 7.0 us)
Async XLA Ops:
  7.2 128.7 %copy-start = (bf16[1,768,512]{2,1,0:T(8,128)(2,1)S(1)}, bf16[1,768,512]{2,1,0:T(8,128)(2,1)}, u32[]{:S(2)}) copy-start(bf16[1,768,512]{2,1,0:T(8,128)(2,1)} %param.13) | copy-start | bytes 2359300
  7.2 97.7 %all-gather.11.cloned.1.call-start = ((), (), s32[]{:S(2)}) async-start(), calls=%async_computation.9 | async-start | bytes 2621440 | tf_op jit(solution)/shard_map/all_gather | solution.py:38
  51.9 70.2 %all-gather.9.cloned.1.call-start = ((), (), s32[]{:S(2)}) async-start(), calls=%async_computation.8 | async-start | bytes 2621440 | tf_op jit(solution)/shard_map/all_gather | solution.py:38
  79.1 1.6 copy-start.2
  79.1 1.7 copy-start.3
  79.1 1.7 copy-start.1
  95.7 26.4 %copy-start.6 = (bf16[1,192,2048]{2,1,0:T(8,128)(2,1)S(1)}, bf16[1,192,2048]{2,1,0:T(8,128)(2,1)}, u32[]{:S(2)}) copy-start(bf16[1,192,2048]{2,1,0:T(8,128)(2,1)} %param.11) | copy-start | bytes 2359300
  95.7 39.8 %all-to-all-start.4 = ((bf16[128,4,2,512]{3,2,1,0:T(2,128)(2,1)}), bf16[128,4,2,512]{3,2,1,0:T(2,128)(2,1)S(1)}, u32[]{:S(2)}, u32[]{:S(2)}) async-start(bf16[128,4,2,512]{3,2,1,0:T(2,128)(2,1)} %copy.58), calls=%async_computation.4 | async-start | bytes 2097152 | tf_op jit(solution)/shard_map/all_to_all | solution.py:63
  104.6 56.1 %all-gather.7.cloned.1.call-start = ((), (), s32[]{:S(2)}) async-start(), calls=%async_computation.6 | async-start | bytes 1966080 | tf_op jit(solution)/shard_map/all_gather | solution.py:79
  122.0 3.9 %copy-start.4 = (bf16[512,1,2048]{2,0,1:T(8,128)(2,1)S(1)}, bf16[512,1,2048]{2,0,1:T(8,128)(2,1)}, u32[]{:S(2)}) copy-start(bf16[512,1,2048]{2,0,1:T(8,128)(2,1)} %all-gather.11.cloned.1.call-done) | copy-start | bytes 6291460
  122.0 3.9 %copy-start.5 = (bf16[512,1,2048]{2,0,1:T(8,128)(2,1)S(1)}, bf16[512,1,2048]{2,0,1:T(8,128)(2,1)}, u32[]{:S(2)}) copy-start(bf16[512,1,2048]{2,0,1:T(8,128)(2,1)} %all-gather.9.cloned.1.call-done) | copy-start | bytes 6291460
  122.1 3.9 %copy-start.7 = (bf16[1,192,2048]{2,1,0:T(8,128)(2,1)S(1)}, bf16[1,192,2048]{2,1,0:T(8,128)(2,1)}, u32[]{:S(2)}) copy-start(bf16[1,192,2048]{2,1,0:T(8,128)(2,1)} %param.12) | copy-start | bytes 2359300
  126.0 2.6 %copy-start.9 = (f32[192,1024]{1,0:T(8,128)}, f32[192,1024]{1,0:T(8,128)S(1)}, u32[]{:S(2)}) copy-start(f32[192,1024]{1,0:T(8,128)S(1)} %convolution_bitcast_fusion.2) | copy-start | bytes 2359300
  128.6 78.6 %reduce-scatter.2.cloned.1.call-start = ((), (), s32[]{:S(2)}) async-start(), calls=%async_computation.7 | async-start | bytes 3932160 | tf_op jit(solution)/shard_map/reduce_scatter | solution.py:87
  165.2 47.0 %all-to-all-start.2 = ((bf16[128,4,2,512]{3,2,1,0:T(2,128)(2,1)}), bf16[128,4,2,512]{3,2,1,0:T(2,128)(2,1)S(1)}, u32[]{:S(2)}, u32[]{:S(2)}) async-start(bf16[128,4,2,512]{3,2,1,0:T(2,128)(2,1)} %bitcast.74), calls=%async_computation.2 | async-start | bytes 2097152 | tf_op jit(solution)/shard_map/all_to_all | solution.py:106
  207.2 9.9 %copy-start.8 = (f32[192,1024]{1,0:T(8,128)S(1)}, f32[192,1024]{1,0:T(8,128)}, u32[]{:S(2)}) copy-start(f32[192,1024]{1,0:T(8,128)} %reduce-scatter.2.cloned.1.call-done) | copy-start | bytes 2359300
  213.8 7.7 %all-to-all-start.3 = ((bf16[4,16,512]{2,1,0:T(8,128)(2,1)}), bf16[4,16,512]{2,1,0:T(8,128)(2,1)S(1)}, u32[]{:S(2)}, u32[]{:S(2)}) async-start(bf16[4,16,512]{2,1,0:T(8,128)(2,1)} %fusion.4), calls=%async_computation.3 | async-start | bytes 131072 | tf_op jit(solution)/shard_map/all_to_all | solution.py:115
Sparse Core Ops, SparseCore 0:
  52.0 28.6 all-gather.10
  83.3 38.6 all-gather.8
  128.7 31.9 all-gather.6
  163.4 43.7 reduce-scatter.1

commit v4 on v2

--- a/solution.py
+++ b/solution.py
@@ -35,12 +35,13 @@
         arrived_input.reshape(experts * capacity, width), "dp", axis=0, tiled=True
     )
 
+    pad = jnp.zeros((tok_rows, 2 * width - 2 * top_count), jnp.float32)
     packed = jnp.concatenate(
-        [cotangent.astype(jnp.float32), routes.astype(jnp.float32), gate_values], axis=1
+        [cotangent.astype(jnp.float32), routes.astype(jnp.float32), gate_values, pad], axis=1
     )
     col = lax.all_gather(packed, "dp", axis=0, tiled=False)
     col_routes = col[:, :, width:width + top_count].astype(jnp.int32)
-    col_gates = col[:, :, width + top_count:]
+    col_gates = col[:, :, width + top_count:width + 2 * top_count]
     me = lax.axis_index("dp")
     cot_q = lax.dynamic_slice_in_dim(col[:, :, :width], me * quarter, quarter, axis=2).astype(
         jnp.bfloat16
@@ -82,13 +83,11 @@
         jnp.bfloat16
     )
     grad_hidden = lax.psum_scatter(
-        lax.dot_general(
-            down_local, cot_quarter, contract_last, preferred_element_type=jnp.float32
-        ).astype(jnp.bfloat16),
+        lax.dot_general(down_local, cot_quarter, contract_last, preferred_element_type=jnp.float32),
         "dp",
         scatter_dimension=0,
         tiled=True,
-    ).astype(jnp.float32)
+    )
     sigma = jax.nn.sigmoid(gate_pre)
     grad_gate = (grad_hidden * up_pre * sigma * (1.0 + gate_pre * (1.0 - sigma))).astype(
         jnp.bfloat16

time: 216 us -> 223 us (1.032)
  waiting for transfers between devices: 78.3 us -> 90.8 us
  blocking collectives: 60.4 us -> 49.1 us
  local copies, waits for them, and re-layouts: 9.6 us -> 13.9 us
    all_gather x1, waiting for transfers between devices: 23.9 us -> 35.6 us  [body(): lax.all_gather(arrived_input.reshape(experts * capacity, width), 'dp', ax...]
    reduce_scatter x1, waiting for transfers between devices: 14.1 us -> 25.6 us  [body(): lax.psum_scatter(lax.dot_general(down_local, cot_quarter, contract_last,...]
    all_gather x1 -> x0, blocking collectives: 11.2 us -> none  [body(): col = lax.all_gather(packed, 'dp', axis=0, tiled=False)]
    all_to_all x1, waiting for transfers between devices: 10.4 us -> 0.01 us  [body(): lax.all_to_all(out_blocks, 'expert', split_axis=0, concat_axis=0, tiled=T...]
  transfers between devices with their start and end apart: 6 -> 7, of which waited for: 5 -> 4; matrix products, arithmetic and copies ran while one was open for 13% -> 17% of each run, Pallas kernels for 0% -> 0%
where the time goes in v4:
time: 223 us; the launch traced here: 222 us
  waiting for transfers between devices  90.8 us (41%)
  blocking collectives  49.1 us (22%)
  matrix products  27.5 us (12%)
  starting transfers between devices  24.4 us (11%)
  between operations  14 us (6%)
  local copies, waits for them, and re-layouts  13.9 us (6%)
  other arithmetic  2.26 us (1%)
    all_to_all x1, blocking collectives, body(): lax.all_to_all(row_input, 'expert', split_axis=0, concat_axis=0, tiled=True)  49.1 us
    all_gather x1, waiting for transfers between devices, body(): lax.all_gather(arrived_input.reshape(experts * capacity, width), 'dp', ax...  35.6 us
    all_gather x1, waiting for transfers between devices, body(): hidden_all = lax.all_gather(hidden_part, 'dp', axis=0, tiled=True)  28.3 us
    reduce_scatter x1, waiting for transfers between devices, body(): lax.psum_scatter(lax.dot_general(down_local, cot_quarter, contract_last,...  25.6 us
    all_to_all x1, starting transfers between devices, body(): lax.all_to_all(out_blocks, 'expert', split_axis=0, concat_axis=0, tiled=T...  14.3 us
    all_to_all x1, starting transfers between devices, body(): lax.all_to_all(row_cot, 'expert', split_axis=0, concat_axis=0, tiled=True)  6.48 us
    dot_general x1, matrix products, body(): jnp.dot(grad_up, inputs_all, preferred_element_type=jnp.float32)  4.71 us
  transfers between devices with their start and end apart: 7, of which 4 were waited for; matrix products, arithmetic and copies ran while one was open for 17% of the time, Pallas kernels for 0%

profile of v4, /device:TPU:1, one launch (start us, length us, event | category | flops | bytes accessed | tf_op | source)
XLA Modules:
  0.0 221.9 jit_solution(5341266160117715413)
XLA Ops:
  8.8 1.7 concatenate.3
  11.6 1.3 convolution_convert_fusion
  12.9 1.1 copy.37
  14.0 49.1 %all_to_all.30 = bf16[128,2,2048]{2,1,0:T(2,128)(2,1)S(1)} all-to-all(bf16[128,2,2048]{2,1,0:T(2,128)(2,1)S(1)} %copy.37), channel_id=1, replica_groups=mesh['dp'=4,'expert'=128] {'expert'}, dimensions={0} | all-to-all | bytes 2097152 | tf_op jit(solution)/shard_map/all_to_all | solution.py:33
  63.1 1.2 reshape.30
  64.4 1.1 slice.14
  67.3 2.1 copy.41
  69.4 6.5 %all-to-all-start.3 = ((bf16[128,4,2,512]{3,2,1,0:T(2,128)(2,1)}), bf16[128,4,2,512]{3,2,1,0:T(2,128)(2,1)S(1)}, u32[]{:S(2)}, u32[]{:S(2)}) async-start(bf16[128,4,2,512]{3,2,1,0:T(2,128)(2,1)} %copy.41), calls=%async_computation.3 | async-start | bytes 2097152 | tf_op jit(solution)/shard_map/all_to_all | solution.py:61
  76.0 35.6 %all-gather.5.cloned.1.call-done = bf16[1024,2048]{1,0:T(8,128)(2,1)} async-done(((bf16[256,2048]{1,0:T(8,128)(2,1)}), bf16[1024,2048]{1,0:T(8,128)(2,1)}) %all-gather.5.cloned.1.call-update) | async-done | bytes 4194320 | tf_op jit(solution)/shard_map/all_gather | solution.py:34
  111.6 3.9 %convolution_bitcast_fusion.2 = f32[192,1024]{1,0:T(8,128)S(1)} fusion(bf16[1024,2048]{1,0:T(8,128)(2,1)} %all-gather.5.cloned.1.call-done, bf16[1,192,2048]{2,1,0:T(8,128)(2,1)S(1)} %copy-done.3), kind=kOutput, calls=%fused_computation.12 | convolution fusion | flops 805306368 | bytes 5767168 | tf_op jit(solution)/shard_map/dot_general | solution.py:70
  115.5 4.1 %multiply_convert_fusion.2 = (bf16[192,1024]{1,0:T(8,128)(2,1)}, f32[192,1024]{1,0:T(8,128)}) fusion(f32[192,1024]{1,0:T(8,128)S(1)} %convolution_bitcast_fusion.2, bf16[1024,2048]{1,0:T(8,128)(2,1)S(1)} %copy-done.1, bf16[1,192,2048]{2,1,0:T(8,128)(2,1)} %param.12), kind=kOutput, calls=%fused_computation.23 | convolution fusion | flops 806486016 | bytes 6946816 | tf_op jit(solution)/shard_map/dot_general | solution.py:73
  121.0 2.7 %convolution_bitcast_fusion = f32[768,1024]{1,0:T(8,128)} fusion(bf16[1024,512]{1,0:T(8,128)(2,1)S(1)} %reshape.32, bf16[1,768,512]{2,1,0:T(8,128)(2,1)S(1)} %copy-done), kind=kOutput, calls=%fused_computation.7 | convolution fusion | flops 805306368 | bytes 4980736 | tf_op jit(solution)/shard_map/dot_general | solution.py:86
  123.8 28.3 %all-gather.7.cloned.1.call-done = bf16[768,1024]{1,0:T(8,128)(2,1)} async-done(((bf16[192,1024]{1,0:T(8,128)(2,1)}), bf16[768,1024]{1,0:T(8,128)(2,1)}) %all-gather.7.cloned.1.call-update) | async-done | bytes 1572880 | tf_op jit(solution)/shard_map/all_gather | solution.py:77
  152.0 3.4 %convolution_convert_fusion.3 = bf16[1024,512]{1,0:T(8,128)(2,1)} fusion(bf16[768,1024]{1,0:T(8,128)(2,1)} %all-gather.7.cloned.1.call-done, bf16[1,768,512]{2,1,0:T(8,128)(2,1)S(1)} %copy-done), kind=kOutput, calls=%fused_computation.8 | convolution fusion | flops 805830656 | bytes 3407872 | tf_op jit(solution)/shard_map/dot_general | solution.py:79
  155.4 1.5 reshape.31
  156.9 1.7 copy.51
  158.6 14.3 %all-to-all-start.1 = ((bf16[128,4,2,512]{3,2,1,0:T(2,128)(2,1)}), bf16[128,4,2,512]{3,2,1,0:T(2,128)(2,1)S(1)}, u32[]{:S(2)}, u32[]{:S(2)}) async-start(bf16[128,4,2,512]{3,2,1,0:T(2,128)(2,1)} %bitcast.72), calls=%async_computation.1 | async-start | bytes 2097152 | tf_op jit(solution)/shard_map/all_to_all | solution.py:104
  172.9 25.6 %reduce-scatter.2.cloned.1.call-done = f32[192,1024]{1,0:T(8,128)} async-done(((f32[768,1024]{1,0:T(8,128)}), f32[192,1024]{1,0:T(8,128)}) %reduce-scatter.2.cloned.1.call-update) | async-done | bytes 786448 | tf_op jit(solution)/shard_map/reduce_scatter | solution.py:85
  198.5 4.7 %fusion.1 = bf16[1,192,2048]{2,1,0:T(8,128)(2,1)} fusion(bf16[1024,2048]{1,0:T(8,128)(2,1)} %all-gather.5.cloned.1.call-done, f32[192,1024]{1,0:T(8,128)} %reduce-scatter.2.cloned.1.call-done, f32[192,1024]{1,0:T(8,128)} %copy-done.5), kind=kOutput, calls=%fused_computation.4 | convolution fusion | flops 806879232 | bytes 6553600 | tf_op jit(solution)/shard_map/dot_general | solution.py:99
  203.3 2.0 fusion
  205.3 1.6 fusion.4
  206.9 3.3 %all-to-all-start.2 = ((bf16[4,16,512]{2,1,0:T(8,128)(2,1)}), bf16[4,16,512]{2,1,0:T(8,128)(2,1)S(1)}, u32[]{:S(2)}, u32[]{:S(2)}) async-start(bf16[4,16,512]{2,1,0:T(8,128)(2,1)} %fusion.4), calls=%async_computation.2 | async-start | bytes 131072 | tf_op jit(solution)/shard_map/all_to_all | solution.py:113
  210.2 3.3 %fusion.3 = bf16[1,768,512]{2,1,0:T(8,128)(2,1)} fusion(bf16[768,1024]{1,0:T(8,128)(2,1)} %all-gather.7.cloned.1.call-done, bf16[1024,512]{1,0:T(8,128)(2,1)S(1)} %reshape.32), kind=kOutput, calls=%fused_computation.10 | convolution fusion | flops 805699584 | bytes 3407872 | tf_op jit(solution)/shard_map/dot_general | solution.py:82
  213.5 1.2 all-to-all-done.2
  (48 shorter events, 6.7 us)
Async XLA Ops:
  7.2 113.9 %copy-start = (bf16[1,768,512]{2,1,0:T(8,128)(2,1)S(1)}, bf16[1,768,512]{2,1,0:T(8,128)(2,1)}, u32[]{:S(2)}) copy-start(bf16[1,768,512]{2,1,0:T(8,128)(2,1)} %param.13) | copy-start | bytes 2359300
  7.2 57.2 %all-gather.9.cloned.1.call-start = ((), (), s32[]{:S(2)}) async-start(), calls=%async_computation.8 | async-start | bytes 1966080 | tf_op jit(solution)/shard_map/all_gather | solution.py:42
  10.6 101.0 %all-gather.5.cloned.1.call-start = ((), (), s32[]{:S(2)}) async-start(), calls=%async_computation.5 | async-start | bytes 5242880 | tf_op jit(solution)/shard_map/all_gather | solution.py:34
  67.3 44.3 %copy-start.3 = (bf16[1,192,2048]{2,1,0:T(8,128)(2,1)S(1)}, bf16[1,192,2048]{2,1,0:T(8,128)(2,1)}, u32[]{:S(2)}) copy-start(bf16[1,192,2048]{2,1,0:T(8,128)(2,1)} %param.11) | copy-start | bytes 2359300
  69.4 50.4 %all-to-all-start.3 = ((bf16[128,4,2,512]{3,2,1,0:T(2,128)(2,1)}), bf16[128,4,2,512]{3,2,1,0:T(2,128)(2,1)S(1)}, u32[]{:S(2)}, u32[]{:S(2)}) async-start(bf16[128,4,2,512]{3,2,1,0:T(2,128)(2,1)} %copy.41), calls=%async_computation.3 | async-start | bytes 2097152 | tf_op jit(solution)/shard_map/all_to_all | solution.py:61
  75.9 76.1 %all-gather.7.cloned.1.call-start = ((), (), s32[]{:S(2)}) async-start(), calls=%async_computation.6 | async-start | bytes 1966080 | tf_op jit(solution)/shard_map/all_gather | solution.py:77
  111.6 3.9 %copy-start.1 = (bf16[1024,2048]{1,0:T(8,128)(2,1)S(1)}, bf16[1024,2048]{1,0:T(8,128)(2,1)}, u32[]{:S(2)}) copy-start(bf16[1024,2048]{1,0:T(8,128)(2,1)} %all-gather.5.cloned.1.call-done) | copy-start | bytes 12582916
  115.5 4.1 %copy-start.5 = (f32[192,1024]{1,0:T(8,128)}, f32[192,1024]{1,0:T(8,128)S(1)}, u32[]{:S(2)}) copy-start(f32[192,1024]{1,0:T(8,128)S(1)} %convolution_bitcast_fusion.2) | copy-start | bytes 2359300
  119.6 78.9 %reduce-scatter.2.cloned.1.call-start = ((), (), s32[]{:S(2)}) async-start(), calls=%async_computation.7 | async-start | bytes 3932160 | tf_op jit(solution)/shard_map/reduce_scatter | solution.py:85
  158.6 46.7 %all-to-all-start.1 = ((bf16[128,4,2,512]{3,2,1,0:T(2,128)(2,1)}), bf16[128,4,2,512]{3,2,1,0:T(2,128)(2,1)S(1)}, u32[]{:S(2)}, u32[]{:S(2)}) async-start(bf16[128,4,2,512]{3,2,1,0:T(2,128)(2,1)} %bitcast.72), calls=%async_computation.1 | async-start | bytes 2097152 | tf_op jit(solution)/shard_map/all_to_all | solution.py:104
  198.5 4.7 %copy-start.2 = (bf16[1024,2048]{1,0:T(8,128)(2,1)S(1)}, bf16[1024,2048]{1,0:T(8,128)(2,1)}, u32[]{:S(2)}) copy-start(bf16[1024,2048]{1,0:T(8,128)(2,1)} %all-gather.5.cloned.1.call-done) | copy-start | bytes 12582916
  198.5 4.7 %copy-start.4 = (f32[192,1024]{1,0:T(8,128)S(1)}, f32[192,1024]{1,0:T(8,128)}, u32[]{:S(2)}) copy-start(f32[192,1024]{1,0:T(8,128)} %reduce-scatter.2.cloned.1.call-done) | copy-start | bytes 2359300
  198.5 4.7 %copy-start.6 = (f32[192,1024]{1,0:T(8,128)S(1)}, f32[192,1024]{1,0:T(8,128)}, u32[]{:S(2)}) copy-start(f32[192,1024]{1,0:T(8,128)} %copy-done.5) | copy-start | bytes 2359300
  198.5 4.7 %copy-start.7 = (f32[192,1024]{1,0:T(8,128)S(1)}, f32[192,1024]{1,0:T(8,128)}, u32[]{:S(2)}) copy-start(f32[192,1024]{1,0:T(8,128)} %get-tuple-element.7) | copy-start | bytes 2359300
  206.9 7.7 %all-to-all-start.2 = ((bf16[4,16,512]{2,1,0:T(8,128)(2,1)}), bf16[4,16,512]{2,1,0:T(8,128)(2,1)S(1)}, u32[]{:S(2)}, u32[]{:S(2)}) async-start(bf16[4,16,512]{2,1,0:T(8,128)(2,1)} %fusion.4), calls=%async_computation.2 | async-start | bytes 131072 | tf_op jit(solution)/shard_map/all_to_all | solution.py:113
Sparse Core Ops, SparseCore 0:
  10.7 37.3 all-gather.8
  64.4 47.1 all-gather.4
  119.7 32.2 all-gather.6
  154.7 43.7 reduce-scatter.1

commit v5 on v1

--- a/solution.py
+++ b/solution.py
@@ -68,7 +68,10 @@
         up_local, inputs_all, contract_last, preferred_element_type=jnp.float32
     )
     hidden_part = (jax.nn.silu(gate_pre) * up_pre).astype(jnp.bfloat16)
-    hidden_all = lax.all_gather(hidden_part, "dp", axis=0, tiled=True)
+    hidden_copies = jnp.broadcast_to(hidden_part[None], (groups,) + hidden_part.shape)
+    hidden_all = lax.all_to_all(hidden_copies, "dp", split_axis=0, concat_axis=0, tiled=True).reshape(
+        groups * hidden_part.shape[0], hidden_part.shape[1]
+    )
     contract_lead = (((0,), (0,)), ((), ()))
     expert_out = lax.dot_general(
         hidden_all, down_local, contract_lead, preferred_element_type=jnp.float32

time: 220 us -> 253 us (1.15)
  blocking collectives: 80.6 us -> 165 us
  waiting for transfers between devices: 57.3 us -> 25.3 us
  starting transfers between devices: 30.6 us -> 10.4 us
    all_to_all x0 -> x2, blocking collectives: none -> 84.4 us  [the longest x1 43.4 us: body(): lax.all_to_all(row_cot, 'expert', split_axis=0, concat_axis=0, tiled=True)]
    reduce_scatter x1, waiting for transfers between devices: 25.7 us -> 0.02 us  [body(): lax.psum_scatter(lax.dot_general(down_local, cot_quarter, contract_last,...]
    all_to_all x1, waiting for transfers between devices: 0.01 us -> 24.1 us  [body(): lax.all_to_all(out_blocks, 'expert', split_axis=0, concat_axis=0, tiled=T...]
    all_to_all x1 -> x0, waiting for transfers between devices: 21.9 us -> none  [body(): lax.all_to_all(row_cot, 'expert', split_axis=0, concat_axis=0, tiled=True)]
    all_to_all x1 -> x0, starting transfers between devices: 12.7 us -> none  [body(): lax.all_to_all(row_cot, 'expert', split_axis=0, concat_axis=0, tiled=True)]
    all_to_all x1, starting transfers between devices: 14.3 us -> 7.02 us  [body(): lax.all_to_all(out_blocks, 'expert', split_axis=0, concat_axis=0, tiled=T...]
    all_gather x1 -> x0, waiting for transfers between devices: 6.24 us -> none  [body(): hidden_all = lax.all_gather(hidden_part, 'dp', axis=0, tiled=True)]
  transfers between devices with their start and end apart: 6 -> 4, of which waited for: 5 -> 2; matrix products, arithmetic and copies ran while one was open for 14% -> 11% of each run, Pallas kernels for 0% -> 0%
where the time goes in v5:
time: 253 us; the launch traced here: 252 us
  blocking collectives  165 us (65%)
  waiting for transfers between devices  25.3 us (10%)
  matrix products  24.5 us (10%)
  between operations  14.3 us (6%)
  local copies, waits for them, and re-layouts  11.9 us (5%)
  starting transfers between devices  10.4 us (4%)
    all_to_all x1, blocking collectives, body(): lax.all_to_all(row_input, 'expert', split_axis=0, concat_axis=0, tiled=True)  49.1 us
    all_to_all x1, blocking collectives, body(): lax.all_to_all(row_cot, 'expert', split_axis=0, concat_axis=0, tiled=True)  43.4 us
    all_to_all x1, blocking collectives, body(): lax.all_to_all(hidden_copies, 'dp', split_axis=0, concat_axis=0, tiled=True)  41 us
    all_to_all x1, waiting for transfers between devices, body(): lax.all_to_all(out_blocks, 'expert', split_axis=0, concat_axis=0, tiled=T...  24.1 us
    all_gather x1, blocking collectives, body(): col_cot = lax.all_gather(cotangent, 'dp', axis=0, tiled=False)  11.8 us
    all_gather x1, blocking collectives, body(): col_gates = lax.all_gather(gate_values, 'dp', axis=0, tiled=False)  10 us
    all_gather x1, blocking collectives, body(): col_routes = lax.all_gather(routes, 'dp', axis=0, tiled=False)  9.39 us
    all_to_all x1, starting transfers between devices, body(): lax.all_to_all(out_blocks, 'expert', split_axis=0, concat_axis=0, tiled=T...  7.02 us
  transfers between devices with their start and end apart: 4, of which 2 were waited for; matrix products, arithmetic and copies ran while one was open for 11% of the time, Pallas kernels for 0%

profile of v5, /device:TPU:1, one launch (start us, length us, event | category | flops | bytes accessed | tf_op | source)
XLA Modules:
  0.0 251.7 jit_solution(8200133805689084541)
XLA Ops:
  8.2 1.3 convolution_convert_fusion
  9.5 1.1 copy.37
  10.6 49.1 %all_to_all.35 = bf16[128,2,2048]{2,1,0:T(2,128)(2,1)S(1)} all-to-all(bf16[128,2,2048]{2,1,0:T(2,128)(2,1)S(1)} %copy.37), channel_id=1, replica_groups=mesh['dp'=4,'expert'=128] {'expert'}, dimensions={0} | all-to-all | bytes 2097152 | tf_op jit(solution)/shard_map/all_to_all | solution.py:33
  59.7 1.3 reshape.34
  61.1 9.4 %all-gather.3 = s32[4,16,8]{1,2,0:T(8,128)S(1)} all-gather(s32[1,16,8]{1,2,0:T(8,128)S(1)} %bitcast.84), channel_id=2, replica_groups=mesh['dp'=4,'expert'=128] {'dp'}, dimensions={0}, use_global_device_ids=true | all-gather | bytes 2560 | tf_op jit(solution)/shard_map/all_gather | solution.py:38
  70.8 10.0 %all-gather.4 = f32[4,16,8]{1,2,0:T(8,128)S(1)} all-gather(f32[1,16,8]{1,2,0:T(8,128)S(1)} %bitcast.85), channel_id=3, replica_groups=mesh['dp'=4,'expert'=128] {'dp'}, dimensions={0}, use_global_device_ids=true | all-gather | bytes 2560 | tf_op jit(solution)/shard_map/all_gather | solution.py:39
  80.8 11.8 %all-gather.2 = bf16[64,2048]{1,0:T(8,128)(2,1)S(1)} all-gather(bf16[16,2048]{1,0:T(8,128)(2,1)S(1)} %copy-done.2), channel_id=4, replica_groups=mesh['dp'=4,'expert'=128] {'dp'}, dimensions={0}, use_global_device_ids=true | all-gather | bytes 327680 | tf_op jit(solution)/shard_map/all_gather | solution.py:40
  94.4 43.4 %all_to_all.36 = bf16[128,4,2,512]{3,2,1,0:T(2,128)(2,1)S(1)} all-to-all(bf16[128,4,2,512]{3,2,1,0:T(2,128)(2,1)S(1)} %copy.41), channel_id=1, replica_groups=mesh['dp'=4,'expert'=128] {'expert'}, dimensions={0} | all-to-all | bytes 2097152 | tf_op jit(solution)/shard_map/all_to_all | solution.py:55
  139.0 2.7 %convolution_bitcast_fusion = f32[768,1024]{1,0:T(8,128)} fusion(bf16[1024,512]{1,0:T(8,128)(2,1)S(1)} %reshape.37, bf16[1,768,512]{2,1,0:T(8,128)(2,1)S(1)} %copy-done), kind=kOutput, calls=%fused_computation.7 | convolution fusion | flops 805306368 | bytes 4980736 | tf_op jit(solution)/shard_map/dot_general | solution.py:83
  142.9 3.9 %convolution_bitcast_fusion.2 = f32[192,1024]{1,0:T(8,128)S(1)} fusion(bf16[1024,2048]{1,0:T(8,128)(2,1)} %all-gather.7.cloned.1.call-done, bf16[1,192,2048]{2,1,0:T(8,128)(2,1)S(1)} %copy-done.7), kind=kOutput, calls=%fused_computation.12 | convolution fusion | flops 805306368 | bytes 5767168 | tf_op jit(solution)/shard_map/dot_general | solution.py:64
  146.8 2.5 multiply_convert_fusion.2
  149.4 41.0 %all_to_all.37 = bf16[4,192,1024]{2,1,0:T(8,128)(2,1)S(1)} all-to-all(bf16[4,192,1024]{2,1,0:T(8,128)(2,1)S(1)} %broadcast_in_dim.22), channel_id=1, replica_groups=mesh['dp'=4,'expert'=128] {'dp'}, dimensions={0} | all-to-all | bytes 3145728 | tf_op jit(solution)/shard_map/all_to_all | solution.py:72
  190.4 1.2 copy-done.1
  191.6 2.0 convolution_convert_fusion.3
  193.7 1.5 reshape.36
  195.1 1.7 copy.51
  196.9 7.0 %all-to-all-start.2 = ((bf16[128,4,2,512]{3,2,1,0:T(2,128)(2,1)}), bf16[128,4,2,512]{3,2,1,0:T(2,128)(2,1)S(1)}, u32[]{:S(2)}, u32[]{:S(2)}) async-start(bf16[128,4,2,512]{3,2,1,0:T(2,128)(2,1)} %bitcast.74), calls=%async_computation.2 | async-start | bytes 2097152 | tf_op jit(solution)/shard_map/all_to_all | solution.py:101
  204.0 4.7 %fusion.1 = bf16[1,192,2048]{2,1,0:T(8,128)(2,1)} fusion(bf16[1024,2048]{1,0:T(8,128)(2,1)} %all-gather.7.cloned.1.call-done, f32[192,1024]{1,0:T(8,128)} %reduce-scatter.2.cloned.1.call-done, f32[192,1024]{1,0:T(8,128)} %copy-done.10), kind=kOutput, calls=%fused_computation.4 | convolution fusion | flops 806879232 | bytes 6553600 | tf_op jit(solution)/shard_map/dot_general | solution.py:96
  208.7 2.0 fusion
  210.7 24.1 %all-to-all-done.2 = bf16[128,4,2,512]{3,2,1,0:T(2,128)(2,1)S(1)} async-done(((bf16[128,4,2,512]{3,2,1,0:T(2,128)(2,1)}), bf16[128,4,2,512]{3,2,1,0:T(2,128)(2,1)S(1)}, u32[]{:S(2)}, u32[]{:S(2)}) %all-to-all-start.2) | async-done | bytes 1048608 | tf_op jit(solution)/shard_map/all_to_all | solution.py:101
  234.8 1.6 fusion.4
  236.5 3.3 %all-to-all-start.3 = ((bf16[4,16,512]{2,1,0:T(8,128)(2,1)}), bf16[4,16,512]{2,1,0:T(8,128)(2,1)S(1)}, u32[]{:S(2)}, u32[]{:S(2)}) async-start(bf16[4,16,512]{2,1,0:T(8,128)(2,1)} %fusion.4), calls=%async_computation.3 | async-start | bytes 131072 | tf_op jit(solution)/shard_map/all_to_all | solution.py:110
  239.7 3.3 %fusion.3 = bf16[1,768,512]{2,1,0:T(8,128)(2,1)} fusion(bf16[768,1024]{1,0:T(8,128)(2,1)} %bitcast.77, bf16[1024,512]{1,0:T(8,128)(2,1)S(1)} %reshape.37), kind=kOutput, calls=%fused_computation.10 | convolution fusion | flops 805699584 | bytes 3407872 | tf_op jit(solution)/shard_map/dot_general | solution.py:79
  243.0 1.2 all-to-all-done.3
  (51 shorter events, 6.4 us)
Async XLA Ops:
  7.2 131.9 %copy-start = (bf16[1,768,512]{2,1,0:T(8,128)(2,1)S(1)}, bf16[1,768,512]{2,1,0:T(8,128)(2,1)}, u32[]{:S(2)}) copy-start(bf16[1,768,512]{2,1,0:T(8,128)(2,1)} %param.13) | copy-start | bytes 2359300
  7.2 134.6 %all-gather.7.cloned.1.call-start = ((), (), s32[]{:S(2)}) async-start(), calls=%async_computation.6 | async-start | bytes 5242880 | tf_op jit(solution)/shard_map/all_gather | solution.py:34
  59.7 1.3 copy-start.3
  59.7 11.0 %copy-start.4 = (f32[16,8]{0,1:T(8,128)S(1)}, f32[16,8]{0,1:T(8,128)}, u32[]{:S(2)}) copy-start(f32[16,8]{0,1:T(8,128)} %param.10) | copy-start | bytes 1540
  59.7 21.1 %copy-start.2 = (bf16[16,2048]{1,0:T(8,128)(2,1)S(1)}, bf16[16,2048]{1,0:T(8,128)(2,1)}, u32[]{:S(2)}) copy-start(bf16[16,2048]{1,0:T(8,128)(2,1)} %param.8) | copy-start | bytes 196612
  61.0 142.9 %reduce-scatter.2.cloned.1.call-start = ((), (), s32[]{:S(2)}) async-start(), calls=%async_computation.7 | async-start | bytes 3932160 | tf_op jit(solution)/shard_map/reduce_scatter | solution.py:82
  141.7 1.1 copy-start.7
  141.7 5.0 %copy-start.8 = (bf16[1,192,2048]{2,1,0:T(8,128)(2,1)S(1)}, bf16[1,192,2048]{2,1,0:T(8,128)(2,1)}, u32[]{:S(2)}) copy-start(bf16[1,192,2048]{2,1,0:T(8,128)(2,1)} %param.12) | copy-start | bytes 2359300
  142.9 3.9 %copy-start.5 = (bf16[1024,2048]{1,0:T(8,128)(2,1)S(1)}, bf16[1024,2048]{1,0:T(8,128)(2,1)}, u32[]{:S(2)}) copy-start(bf16[1024,2048]{1,0:T(8,128)(2,1)} %all-gather.7.cloned.1.call-done) | copy-start | bytes 12582916
  146.7 2.5 copy-start.10
  190.4 1.2 copy-start.1
  196.9 37.9 %all-to-all-start.2 = ((bf16[128,4,2,512]{3,2,1,0:T(2,128)(2,1)}), bf16[128,4,2,512]{3,2,1,0:T(2,128)(2,1)S(1)}, u32[]{:S(2)}, u32[]{:S(2)}) async-start(bf16[128,4,2,512]{3,2,1,0:T(2,128)(2,1)} %bitcast.74), calls=%async_computation.2 | async-start | bytes 2097152 | tf_op jit(solution)/shard_map/all_to_all | solution.py:101
  203.9 4.8 %copy-start.6 = (bf16[1024,2048]{1,0:T(8,128)(2,1)S(1)}, bf16[1024,2048]{1,0:T(8,128)(2,1)}, u32[]{:S(2)}) copy-start(bf16[1024,2048]{1,0:T(8,128)(2,1)} %all-gather.7.cloned.1.call-done) | copy-start | bytes 12582916
  203.9 4.8 %copy-start.9 = (f32[192,1024]{1,0:T(8,128)S(1)}, f32[192,1024]{1,0:T(8,128)}, u32[]{:S(2)}) copy-start(f32[192,1024]{1,0:T(8,128)} %reduce-scatter.2.cloned.1.call-done) | copy-start | bytes 2359300
  204.0 4.7 %copy-start.11 = (f32[192,1024]{1,0:T(8,128)S(1)}, f32[192,1024]{1,0:T(8,128)}, u32[]{:S(2)}) copy-start(f32[192,1024]{1,0:T(8,128)} %copy-done.10) | copy-start | bytes 2359300
  204.0 4.7 %copy-start.12 = (f32[192,1024]{1,0:T(8,128)S(1)}, f32[192,1024]{1,0:T(8,128)}, u32[]{:S(2)}) copy-start(f32[192,1024]{1,0:T(8,128)} %get-tuple-element.5) | copy-start | bytes 2359300
  236.5 7.7 %all-to-all-start.3 = ((bf16[4,16,512]{2,1,0:T(8,128)(2,1)}), bf16[4,16,512]{2,1,0:T(8,128)(2,1)S(1)}, u32[]{:S(2)}, u32[]{:S(2)}) async-start(bf16[4,16,512]{2,1,0:T(8,128)(2,1)} %fusion.4), calls=%async_computation.3 | async-start | bytes 131072 | tf_op jit(solution)/shard_map/all_to_all | solution.py:110
Sparse Core Ops, SparseCore 0:
  61.1 49.3 all-gather.6
  141.9 53.4 reduce-scatter.1

commit v6 on v1

--- a/solution.py
+++ b/solution.py
@@ -82,6 +82,17 @@
         scatter_dimension=0,
         tiled=True,
     )
+    out_blocks = jnp.transpose(expert_out.reshape(groups, experts, capacity, quarter), (1, 0, 2, 3))
+    returned = lax.all_to_all(out_blocks, "expert", split_axis=0, concat_axis=0, tiled=True)
+    combine = col_placer.astype(jnp.float32) * col_slot_gate[:, :, :, None]
+    mixed_q = jnp.einsum(
+        "gest,egsd->gtd",
+        combine,
+        returned.astype(jnp.float32),
+        precision=lax.Precision.HIGHEST,
+        preferred_element_type=jnp.float32,
+    ).astype(jnp.bfloat16)
+    grad_hidden, mixed_q = lax.optimization_barrier((grad_hidden, mixed_q))
     sigma = jax.nn.sigmoid(gate_pre)
     grad_gate = (grad_hidden * up_pre * sigma * (1.0 + gate_pre * (1.0 - sigma))).astype(
         jnp.bfloat16
@@ -94,16 +105,6 @@
         jnp.bfloat16
     )
 
-    out_blocks = jnp.transpose(expert_out.reshape(groups, experts, capacity, quarter), (1, 0, 2, 3))
-    returned = lax.all_to_all(out_blocks, "expert", split_axis=0, concat_axis=0, tiled=True)
-    combine = col_placer.astype(jnp.float32) * col_slot_gate[:, :, :, None]
-    mixed_q = jnp.einsum(
-        "gest,egsd->gtd",
-        combine,
-        returned.astype(jnp.float32),
-        precision=lax.Precision.HIGHEST,
-        preferred_element_type=jnp.float32,
-    ).astype(jnp.bfloat16)
     mixed = lax.all_to_all(mixed_q, "dp", split_axis=0, concat_axis=2, tiled=True)
     return (mixed[0], grad_gate_local[None], grad_up_local[None], grad_down[None])
 

time: 220 us -> 223 us (1.014)
  local copies, waits for them, and re-layouts: 10.5 us -> 15.9 us
  waiting for transfers between devices: 57.3 us -> 52.5 us
    reduce_scatter x1 -> x0, waiting for transfers between devices: 25.7 us -> none  [body(): lax.psum_scatter(lax.dot_general(down_local, cot_quarter, contract_last,...]
    unnamed x3 -> x4, waiting for transfers between devices: 0.05 us -> 25.3 us
    all_gather x1, waiting for transfers between devices: 6.24 us -> 2.58 us  [body(): hidden_all = lax.all_gather(hidden_part, 'dp', axis=0, tiled=True)]
    unnamed x26 -> x23, local copies, waits for them, and re-layouts: 1.53 us -> 5.13 us
    dot_general x1, matrix products: 2.04 us -> 4.8 us  [body(): jnp.dot(grad_gate, inputs_all, preferred_element_type=jnp.float32)]
    dot_general x1, matrix products: 4.71 us -> 1.95 us  [body(): jnp.dot(grad_up, inputs_all, preferred_element_type=jnp.float32)]
  transfers between devices with their start and end apart: 6 -> 6, of which waited for: 5 -> 5; matrix products, arithmetic and copies ran while one was open for 14% -> 16% of each run, Pallas kernels for 0% -> 0%
where the time goes in v6:
time: 223 us; the launch traced here: 222 us
  blocking collectives  80.6 us (36%)
  waiting for transfers between devices  52.5 us (24%)
  starting transfers between devices  31.1 us (14%)
  matrix products  27.3 us (12%)
  local copies, waits for them, and re-layouts  15.9 us (7%)
  between operations  14 us (6%)
    all_to_all x1, blocking collectives, body(): lax.all_to_all(row_input, 'expert', split_axis=0, concat_axis=0, tiled=True)  49.3 us
    unnamed x4, waiting for transfers between devices  25.3 us
    all_to_all x1, waiting for transfers between devices, body(): lax.all_to_all(row_cot, 'expert', split_axis=0, concat_axis=0, tiled=True)  22 us
    all_to_all x1, starting transfers between devices, body(): lax.all_to_all(out_blocks, 'expert', split_axis=0, concat_axis=0, tiled=T...  14.8 us
    all_to_all x1, starting transfers between devices, body(): lax.all_to_all(row_cot, 'expert', split_axis=0, concat_axis=0, tiled=True)  12.7 us
    all_gather x1, blocking collectives, body(): col_cot = lax.all_gather(cotangent, 'dp', axis=0, tiled=False)  11.8 us
    all_gather x1, blocking collectives, body(): col_routes = lax.all_gather(routes, 'dp', axis=0, tiled=False)  10 us
    all_gather x1, blocking collectives, body(): col_gates = lax.all_gather(gate_values, 'dp', axis=0, tiled=False)  9.52 us
  transfers between devices with their start and end apart: 6, of which 5 were waited for; matrix products, arithmetic and copies ran while one was open for 16% of the time, Pallas kernels for 0%

profile of v6, /device:TPU:1, one launch (start us, length us, event | category | flops | bytes accessed | tf_op | source)
XLA Modules:
  0.0 222.0 jit_solution(10173116045346307721)
XLA Ops:
  10.6 49.3 %all_to_all.30 = bf16[128,2,2048]{2,1,0:T(2,128)(2,1)S(1)} all-to-all(bf16[128,2,2048]{2,1,0:T(2,128)(2,1)S(1)} %copy.42), channel_id=1, replica_groups=mesh['dp'=4,'expert'=128] {'expert'}, dimensions={0} | all-to-all | bytes 2097152 | tf_op jit(solution)/shard_map/all_to_all | solution.py:33
  61.2 9.5 %all-gather.4 = f32[4,16,8]{1,2,0:T(8,128)S(1)} all-gather(f32[1,16,8]{1,2,0:T(8,128)S(1)} %bitcast.82), channel_id=3, replica_groups=mesh['dp'=4,'expert'=128] {'dp'}, dimensions={0}, use_global_device_ids=true | all-gather | bytes 2560 | tf_op jit(solution)/shard_map/all_gather | solution.py:39
  70.8 10.0 %all-gather.3 = s32[4,16,8]{1,2,0:T(8,128)S(1)} all-gather(s32[1,16,8]{1,2,0:T(8,128)S(1)} %bitcast.81), channel_id=2, replica_groups=mesh['dp'=4,'expert'=128] {'dp'}, dimensions={0}, use_global_device_ids=true | all-gather | bytes 2560 | tf_op jit(solution)/shard_map/all_gather | solution.py:38
  81.0 11.8 %all-gather.2 = bf16[64,2048]{1,0:T(8,128)(2,1)S(1)} all-gather(bf16[16,2048]{1,0:T(8,128)(2,1)S(1)} %copy-done.1), channel_id=4, replica_groups=mesh['dp'=4,'expert'=128] {'dp'}, dimensions={0}, use_global_device_ids=true | all-gather | bytes 327680 | tf_op jit(solution)/shard_map/all_gather | solution.py:40
  93.6 2.1 copy.39
  95.7 12.7 %all-to-all-start = ((bf16[128,4,2,512]{3,2,1,0:T(2,128)(2,1)}), bf16[128,4,2,512]{3,2,1,0:T(2,128)(2,1)S(1)}, u32[]{:S(2)}, u32[]{:S(2)}) async-start(bf16[128,4,2,512]{3,2,1,0:T(2,128)(2,1)} %copy.39), calls=%async_computation | async-start | bytes 2097152 | tf_op jit(solution)/shard_map/all_to_all | solution.py:55
  108.5 2.1 all-gather.8.cloned.1.call-done
  110.7 3.9 %convolution_bitcast_fusion.2 = f32[192,1024]{1,0:T(8,128)S(1)} fusion(bf16[1024,2048]{1,0:T(8,128)(2,1)} %all-gather.8.cloned.1.call-done, bf16[1,192,2048]{2,1,0:T(8,128)(2,1)S(1)} %copy-done.6), kind=kOutput, calls=%fused_computation.12 | convolution fusion | flops 805306368 | bytes 5767168 | tf_op jit(solution)/shard_map/dot_general | solution.py:64
  114.6 2.6 %multiply_convert_fusion.2 = (bf16[192,1024]{1,0:T(8,128)(2,1)}, f32[192,1024]{1,0:T(8,128)}) fusion(f32[192,1024]{1,0:T(8,128)S(1)} %convolution_bitcast_fusion.2, bf16[1024,2048]{1,0:T(8,128)(2,1)S(1)} %copy-done.4, bf16[1,192,2048]{2,1,0:T(8,128)(2,1)S(1)} %copy-done.7), kind=kOutput, calls=%fused_computation.23 | convolution fusion | flops 806486016 | bytes 6946816 | tf_op jit(solution)/shard_map/dot_general | solution.py:67
  117.4 22.0 %all-to-all-done = bf16[128,4,2,512]{3,2,1,0:T(2,128)(2,1)S(1)} async-done(((bf16[128,4,2,512]{3,2,1,0:T(2,128)(2,1)}), bf16[128,4,2,512]{3,2,1,0:T(2,128)(2,1)S(1)}, u32[]{:S(2)}, u32[]{:S(2)}) %all-to-all-start) | async-done | bytes 1048608 | tf_op jit(solution)/shard_map/all_to_all | solution.py:55
  140.5 2.7 %convolution_bitcast_fusion = f32[768,1024]{0,1:T(8,128)} fusion(bf16[1024,512]{1,0:T(8,128)(2,1)S(1)} %reshape.30, bf16[1,768,512]{2,1,0:T(8,128)(2,1)S(1)} %copy-done), kind=kOutput, calls=%fused_computation.7 | convolution fusion | flops 805306368 | bytes 4980736 | tf_op jit(solution)/shard_map/dot_general | solution.py:80
  143.3 3.6 %copy.50 = f32[768,1024]{1,0:T(8,128)} copy(f32[768,1024]{0,1:T(8,128)} %convolution_bitcast_fusion) | data formatting | bytes 6291456
  146.9 2.6 %all-gather.10.cloned.1.call-done = bf16[768,1024]{1,0:T(8,128)(2,1)} async-done(((bf16[192,1024]{1,0:T(8,128)(2,1)}), bf16[768,1024]{1,0:T(8,128)(2,1)}) %all-gather.10.cloned.1.call-update) | async-done | bytes 1572880 | tf_op jit(solution)/shard_map/all_gather | solution.py:71
  149.5 3.4 %convolution_convert_fusion.3 = bf16[1024,512]{1,0:T(8,128)(2,1)} fusion(bf16[768,1024]{1,0:T(8,128)(2,1)} %all-gather.10.cloned.1.call-done, bf16[1,768,512]{2,1,0:T(8,128)(2,1)S(1)} %copy-done), kind=kOutput, calls=%fused_computation.8 | convolution fusion | flops 805830656 | bytes 3407872 | tf_op jit(solution)/shard_map/dot_general | solution.py:73
  152.9 1.5 reshape.32
  154.4 1.8 copy.56
  156.2 14.8 %all-to-all-start.2 = ((bf16[128,4,2,512]{3,2,1,0:T(2,128)(2,1)}), bf16[128,4,2,512]{3,2,1,0:T(2,128)(2,1)}, u32[]{:S(2)}, u32[]{:S(2)}) async-start(bf16[128,4,2,512]{3,2,1,0:T(2,128)(2,1)} %bitcast.73), calls=%async_computation.2 | async-start | bytes 2097152 | tf_op jit(solution)/shard_map/all_to_all | solution.py:86
  170.9 25.2 %reduce-scatter.4.cloned.1.call-done = f32[192,1024]{1,0:T(8,128)} async-done(((f32[768,1024]{1,0:T(8,128)}), f32[192,1024]{1,0:T(8,128)}) %reduce-scatter.4.cloned.1.call-update) | async-done | bytes 786448
  196.1 1.5 copy.51
  197.6 3.3 %fusion.3 = bf16[1,768,512]{2,1,0:T(8,128)(2,1)} fusion(bf16[768,1024]{1,0:T(8,128)(2,1)} %all-gather.10.cloned.1.call-done, bf16[1024,512]{1,0:T(8,128)(2,1)S(1)} %reshape.30), kind=kOutput, calls=%fused_computation.10 | convolution fusion | flops 805699584 | bytes 3407872 | tf_op jit(solution)/shard_map/dot_general | solution.py:76
  201.5 2.9 %fusion.4 = bf16[4,16,512]{2,1,0:T(8,128)(2,1)} fusion(bf16[128,4,2,512]{3,2,1,0:T(2,128)(2,1)} %all-to-all-done.2, f32[4,128,2]{1,2,0:T(2,128)S(1)} %select_reduce_fusion.1, s32[4,128,16]{1,2,0:T(8,128)S(1)} %subtract_bitcast_fusion, pred[4,128,16]{1,2,0:T(8,128)(4,1)S(1)} %compare_bitcast_fusion), kind=kOutput, calls=%fused_computation.14 | convolution fusion | flops 100745216 | bytes 1159168 | tf_op jit(solution)/shard_map/gest,egsd->gtd/dot_general | solution.py:88
  204.3 3.3 %all-to-all-start.3 = ((bf16[4,16,512]{2,1,0:T(8,128)(2,1)}), bf16[4,16,512]{2,1,0:T(8,128)(2,1)S(1)}, u32[]{:S(2)}, u32[]{:S(2)}) async-start(bf16[4,16,512]{2,1,0:T(8,128)(2,1)} %fusion.4), calls=%async_computation.3 | async-start | bytes 131072 | tf_op jit(solution)/shard_map/all_to_all | solution.py:108
  208.0 4.8 %fusion = bf16[1,192,2048]{2,1,0:T(8,128)(2,1)} fusion(bf16[1024,2048]{1,0:T(8,128)(2,1)} %all-gather.8.cloned.1.call-done, f32[192,1024]{1,0:T(8,128)} %copy-done.8, f32[192,1024]{1,0:T(8,128)S(1)} %copy.46, f32[192,1024]{1,0:T(8,128)} %get-tuple-element.9), kind=kOutput, calls=%fused_computation.3 | convolution fusion | flops 807665664 | bytes 7340032 | tf_op jit(solution)/shard_map/dot_general | solution.py:101
  212.8 2.0 fusion.1
  (50 shorter events, 8.8 us)
Async XLA Ops:
  7.2 133.4 %copy-start = (bf16[1,768,512]{2,1,0:T(8,128)(2,1)S(1)}, bf16[1,768,512]{2,1,0:T(8,128)(2,1)}, u32[]{:S(2)}) copy-start(bf16[1,768,512]{2,1,0:T(8,128)(2,1)} %param.13) | copy-start | bytes 2359300
  7.2 103.5 %all-gather.8.cloned.1.call-start = ((), (), s32[]{:S(2)}) async-start(), calls=%async_computation.5 | async-start | bytes 5242880 | tf_op jit(solution)/shard_map/all_gather | solution.py:34
  10.6 50.5 %copy-start.3 = (f32[16,8]{0,1:T(8,128)S(1)}, f32[16,8]{0,1:T(8,128)}, u32[]{:S(2)}) copy-start(f32[16,8]{0,1:T(8,128)} %param.10) | copy-start | bytes 1540
  10.6 60.1 %copy-start.2 = (s32[16,8]{0,1:T(8,128)S(1)}, s32[16,8]{0,1:T(8,128)}, u32[]{:S(2)}) copy-start(s32[16,8]{0,1:T(8,128)} %param.9) | copy-start | bytes 1540
  10.6 70.4 %copy-start.1 = (bf16[16,2048]{1,0:T(8,128)(2,1)S(1)}, bf16[16,2048]{1,0:T(8,128)(2,1)}, u32[]{:S(2)}) copy-start(bf16[16,2048]{1,0:T(8,128)(2,1)} %param.8) | copy-start | bytes 196612
  61.1 49.5 %copy-start.6 = (bf16[1,192,2048]{2,1,0:T(8,128)(2,1)S(1)}, bf16[1,192,2048]{2,1,0:T(8,128)(2,1)}, u32[]{:S(2)}) copy-start(bf16[1,192,2048]{2,1,0:T(8,128)(2,1)} %param.11) | copy-start | bytes 2359300
  95.7 43.6 %all-to-all-start = ((bf16[128,4,2,512]{3,2,1,0:T(2,128)(2,1)}), bf16[128,4,2,512]{3,2,1,0:T(2,128)(2,1)S(1)}, u32[]{:S(2)}, u32[]{:S(2)}) async-start(bf16[128,4,2,512]{3,2,1,0:T(2,128)(2,1)} %copy.39), calls=%async_computation | async-start | bytes 2097152 | tf_op jit(solution)/shard_map/all_to_all | solution.py:55
  108.5 6.1 %copy-start.7 = (bf16[1,192,2048]{2,1,0:T(8,128)(2,1)S(1)}, bf16[1,192,2048]{2,1,0:T(8,128)(2,1)}, u32[]{:S(2)}) copy-start(bf16[1,192,2048]{2,1,0:T(8,128)(2,1)} %param.12) | copy-start | bytes 2359300
  108.5 41.0 %all-gather.10.cloned.1.call-start = ((), (), s32[]{:S(2)}) async-start(), calls=%async_computation.6 | async-start | bytes 1966080 | tf_op jit(solution)/shard_map/all_gather | solution.py:71
  110.7 3.9 %copy-start.4 = (bf16[1024,2048]{1,0:T(8,128)(2,1)S(1)}, bf16[1024,2048]{1,0:T(8,128)(2,1)}, u32[]{:S(2)}) copy-start(bf16[1024,2048]{1,0:T(8,128)(2,1)} %all-gather.8.cloned.1.call-done) | copy-start | bytes 12582916
  114.5 2.6 %copy-start.8 = (f32[192,1024]{1,0:T(8,128)}, f32[192,1024]{1,0:T(8,128)S(1)}, u32[]{:S(2)}) copy-start(f32[192,1024]{1,0:T(8,128)S(1)} %convolution_bitcast_fusion.2) | copy-start | bytes 2359300
  117.2 79.0 %reduce-scatter.4.cloned.1.call-start = ((), (), s32[]{:S(2)}) async-start(), calls=%async_computation.7 | async-start | bytes 3932160
  156.2 45.3 %all-to-all-start.2 = ((bf16[128,4,2,512]{3,2,1,0:T(2,128)(2,1)}), bf16[128,4,2,512]{3,2,1,0:T(2,128)(2,1)}, u32[]{:S(2)}, u32[]{:S(2)}) async-start(bf16[128,4,2,512]{3,2,1,0:T(2,128)(2,1)} %bitcast.73), calls=%async_computation.2 | async-start | bytes 2097152 | tf_op jit(solution)/shard_map/all_to_all | solution.py:86
  204.3 10.4 %all-to-all-start.3 = ((bf16[4,16,512]{2,1,0:T(8,128)(2,1)}), bf16[4,16,512]{2,1,0:T(8,128)(2,1)S(1)}, u32[]{:S(2)}, u32[]{:S(2)}) async-start(bf16[4,16,512]{2,1,0:T(8,128)(2,1)} %fusion.4), calls=%async_computation.3 | async-start | bytes 131072 | tf_op jit(solution)/shard_map/all_to_all | solution.py:108
  207.9 4.8 %copy-start.5 = (bf16[1024,2048]{1,0:T(8,128)(2,1)S(1)}, bf16[1024,2048]{1,0:T(8,128)(2,1)}, u32[]{:S(2)}) copy-start(bf16[1024,2048]{1,0:T(8,128)(2,1)} %all-gather.8.cloned.1.call-done) | copy-start | bytes 12582916
  208.0 4.8 %copy-start.9 = (f32[192,1024]{1,0:T(8,128)S(1)}, f32[192,1024]{1,0:T(8,128)}, u32[]{:S(2)}) copy-start(f32[192,1024]{1,0:T(8,128)} %copy-done.8) | copy-start | bytes 2359300
Sparse Core Ops, SparseCore 0:
  61.2 49.3 all-gather.7
  117.3 32.1 all-gather.9
  152.3 43.7 reduce-scatter.3

commit v7 on v1

--- a/solution.py
+++ b/solution.py
@@ -95,6 +95,7 @@
     )
 
     out_blocks = jnp.transpose(expert_out.reshape(groups, experts, capacity, quarter), (1, 0, 2, 3))
+    out_blocks, grad_down = lax.optimization_barrier((out_blocks, grad_down))
     returned = lax.all_to_all(out_blocks, "expert", split_axis=0, concat_axis=0, tiled=True)
     combine = col_placer.astype(jnp.float32) * col_slot_gate[:, :, :, None]
     mixed_q = jnp.einsum(

time: 220 us -> 223 us (1.014)
  matrix products: 26 us -> 28.3 us
    all_to_all x1, waiting for transfers between devices: 0.01 us -> 3.76 us  [body(): lax.all_to_all(out_blocks, 'expert', split_axis=0, concat_axis=0, tiled=T...]
    reduce_scatter x1, waiting for transfers between devices: 25.7 us -> 22.4 us  [body(): lax.psum_scatter(lax.dot_general(down_local, cot_quarter, contract_last,...]
    dot_general x1, matrix products: 2.04 us -> 4.78 us  [body(): jnp.dot(grad_gate, inputs_all, preferred_element_type=jnp.float32)]
  transfers between devices with their start and end apart: 6 -> 6, of which waited for: 5 -> 6; matrix products, arithmetic and copies ran while one was open for 14% -> 15% of each run, Pallas kernels for 0% -> 0%
where the time goes in v7:
time: 223 us; the launch traced here: 221 us
  blocking collectives  80.6 us (36%)
  waiting for transfers between devices  56.8 us (25%)
  starting transfers between devices  30.6 us (14%)
  matrix products  28.3 us (13%)
  between operations  14 us (6%)
  local copies, waits for them, and re-layouts  10.5 us (5%)
    all_to_all x1, blocking collectives, body(): lax.all_to_all(row_input, 'expert', split_axis=0, concat_axis=0, tiled=True)  49.3 us
    reduce_scatter x1, waiting for transfers between devices, body(): lax.psum_scatter(lax.dot_general(down_local, cot_quarter, contract_last,...  22.4 us
    all_to_all x1, waiting for transfers between devices, body(): lax.all_to_all(row_cot, 'expert', split_axis=0, concat_axis=0, tiled=True)  22 us
    all_to_all x1, starting transfers between devices, body(): lax.all_to_all(out_blocks, 'expert', split_axis=0, concat_axis=0, tiled=T...  14.3 us
    all_to_all x1, starting transfers between devices, body(): lax.all_to_all(row_cot, 'expert', split_axis=0, concat_axis=0, tiled=True)  12.7 us
    all_gather x1, blocking collectives, body(): col_cot = lax.all_gather(cotangent, 'dp', axis=0, tiled=False)  11.8 us
    all_gather x1, blocking collectives, body(): col_routes = lax.all_gather(routes, 'dp', axis=0, tiled=False)  10 us
    all_gather x1, blocking collectives, body(): col_gates = lax.all_gather(gate_values, 'dp', axis=0, tiled=False)  9.52 us
  transfers between devices with their start and end apart: 6, of which 6 were waited for; matrix products, arithmetic and copies ran while one was open for 15% of the time, Pallas kernels for 0%

profile of v7, /device:TPU:1, one launch (start us, length us, event | category | flops | bytes accessed | tf_op | source)
XLA Modules:
  0.0 221.3 jit_solution(4514497862034653932)
XLA Ops:
  8.2 1.3 convolution_convert_fusion
  10.6 49.3 %all_to_all.30 = bf16[128,2,2048]{2,1,0:T(2,128)(2,1)S(1)} all-to-all(bf16[128,2,2048]{2,1,0:T(2,128)(2,1)S(1)} %copy.37), channel_id=1, replica_groups=mesh['dp'=4,'expert'=128] {'expert'}, dimensions={0} | all-to-all | bytes 2097152 | tf_op jit(solution)/shard_map/all_to_all | solution.py:33
  61.2 9.5 %all-gather.4 = f32[4,16,8]{1,2,0:T(8,128)S(1)} all-gather(f32[1,16,8]{1,2,0:T(8,128)S(1)} %bitcast.80), channel_id=3, replica_groups=mesh['dp'=4,'expert'=128] {'dp'}, dimensions={0}, use_global_device_ids=true | all-gather | bytes 2560 | tf_op jit(solution)/shard_map/all_gather | solution.py:39
  70.8 10.0 %all-gather.3 = s32[4,16,8]{1,2,0:T(8,128)S(1)} all-gather(s32[1,16,8]{1,2,0:T(8,128)S(1)} %bitcast.79), channel_id=2, replica_groups=mesh['dp'=4,'expert'=128] {'dp'}, dimensions={0}, use_global_device_ids=true | all-gather | bytes 2560 | tf_op jit(solution)/shard_map/all_gather | solution.py:38
  81.0 11.8 %all-gather.2 = bf16[64,2048]{1,0:T(8,128)(2,1)S(1)} all-gather(bf16[16,2048]{1,0:T(8,128)(2,1)S(1)} %copy-done.1), channel_id=4, replica_groups=mesh['dp'=4,'expert'=128] {'dp'}, dimensions={0}, use_global_device_ids=true | all-gather | bytes 327680 | tf_op jit(solution)/shard_map/all_gather | solution.py:40
  93.6 2.1 copy.39
  95.7 12.7 %all-to-all-start.1 = ((bf16[128,4,2,512]{3,2,1,0:T(2,128)(2,1)}), bf16[128,4,2,512]{3,2,1,0:T(2,128)(2,1)S(1)}, u32[]{:S(2)}, u32[]{:S(2)}) async-start(bf16[128,4,2,512]{3,2,1,0:T(2,128)(2,1)} %copy.39), calls=%async_computation.1 | async-start | bytes 2097152 | tf_op jit(solution)/shard_map/all_to_all | solution.py:55
  108.5 2.1 all-gather.8.cloned.1.call-done
  110.7 3.9 %convolution_bitcast_fusion.2 = f32[192,1024]{1,0:T(8,128)S(1)} fusion(bf16[1024,2048]{1,0:T(8,128)(2,1)} %all-gather.8.cloned.1.call-done, bf16[1,192,2048]{2,1,0:T(8,128)(2,1)S(1)} %copy-done.5), kind=kOutput, calls=%fused_computation.11 | convolution fusion | flops 805306368 | bytes 5767168 | tf_op jit(solution)/shard_map/dot_general | solution.py:64
  114.6 2.6 %multiply_convert_fusion.2 = (bf16[192,1024]{1,0:T(8,128)(2,1)}, f32[192,1024]{1,0:T(8,128)}) fusion(f32[192,1024]{1,0:T(8,128)S(1)} %convolution_bitcast_fusion.2, bf16[1024,2048]{1,0:T(8,128)(2,1)S(1)} %copy-done.4, bf16[1,192,2048]{2,1,0:T(8,128)(2,1)S(1)} %copy-done.6), kind=kOutput, calls=%fused_computation.22 | convolution fusion | flops 806486016 | bytes 6946816 | tf_op jit(solution)/shard_map/dot_general | solution.py:67
  117.4 22.0 %all-to-all-done.1 = bf16[128,4,2,512]{3,2,1,0:T(2,128)(2,1)S(1)} async-done(((bf16[128,4,2,512]{3,2,1,0:T(2,128)(2,1)}), bf16[128,4,2,512]{3,2,1,0:T(2,128)(2,1)S(1)}, u32[]{:S(2)}, u32[]{:S(2)}) %all-to-all-start.1) | async-done | bytes 1048608 | tf_op jit(solution)/shard_map/all_to_all | solution.py:55
  140.5 2.7 %convolution_bitcast_fusion = f32[768,1024]{1,0:T(8,128)} fusion(bf16[1024,512]{1,0:T(8,128)(2,1)S(1)} %reshape.32, bf16[1,768,512]{2,1,0:T(8,128)(2,1)S(1)} %copy-done), kind=kOutput, calls=%fused_computation.7 | convolution fusion | flops 805306368 | bytes 4980736 | tf_op jit(solution)/shard_map/dot_general | solution.py:80
  143.3 6.2 %all-gather.10.cloned.1.call-done = bf16[768,1024]{1,0:T(8,128)(2,1)} async-done(((bf16[192,1024]{1,0:T(8,128)(2,1)}), bf16[768,1024]{1,0:T(8,128)(2,1)}) %all-gather.10.cloned.1.call-update) | async-done | bytes 1572880 | tf_op jit(solution)/shard_map/all_gather | solution.py:71
  149.5 3.4 %convolution_convert_fusion.3 = bf16[1024,512]{1,0:T(8,128)(2,1)} fusion(bf16[768,1024]{1,0:T(8,128)(2,1)} %all-gather.10.cloned.1.call-done, bf16[1,768,512]{2,1,0:T(8,128)(2,1)S(1)} %copy-done), kind=kOutput, calls=%fused_computation.8 | convolution fusion | flops 805830656 | bytes 3407872 | tf_op jit(solution)/shard_map/dot_general | solution.py:73
  152.9 1.5 reshape.31
  154.4 1.7 copy.51
  156.1 3.3 %convolution_convert_fusion.4 = bf16[768,512]{1,0:T(8,128)(2,1)} fusion(bf16[768,1024]{1,0:T(8,128)(2,1)} %all-gather.10.cloned.1.call-done, bf16[1024,512]{1,0:T(8,128)(2,1)S(1)} %reshape.32), kind=kOutput, calls=%fused_computation.9 | convolution fusion | flops 805699584 | bytes 3407872 | tf_op jit(solution)/shard_map/dot_general | solution.py:76
  159.5 14.3 %all-to-all-start.2 = ((bf16[128,4,2,512]{3,2,1,0:T(2,128)(2,1)}), bf16[128,4,2,512]{3,2,1,0:T(2,128)(2,1)S(1)}, u32[]{:S(2)}, u32[]{:S(2)}) async-start(bf16[128,4,2,512]{3,2,1,0:T(2,128)(2,1)} %bitcast.71), calls=%async_computation.2 | async-start | bytes 2097152 | tf_op jit(solution)/shard_map/all_to_all | solution.py:99
  173.8 22.4 %reduce-scatter.2.cloned.1.call-done = f32[192,1024]{1,0:T(8,128)} async-done(((f32[768,1024]{1,0:T(8,128)}), f32[192,1024]{1,0:T(8,128)}) %reduce-scatter.2.cloned.1.call-update) | async-done | bytes 786448 | tf_op jit(solution)/shard_map/reduce_scatter | solution.py:79
  196.2 4.8 %fusion = bf16[1,192,2048]{2,1,0:T(8,128)(2,1)} fusion(bf16[1024,2048]{1,0:T(8,128)(2,1)} %all-gather.8.cloned.1.call-done, f32[192,1024]{1,0:T(8,128)S(1)} %copy-done.9, f32[192,1024]{1,0:T(8,128)} %reduce-scatter.2.cloned.1.call-done, f32[192,1024]{1,0:T(8,128)} %get-tuple-element.9), kind=kOutput, calls=%fused_computation.3 | convolution fusion | flops 807665664 | bytes 7340032 | tf_op jit(solution)/shard_map/dot_general | solution.py:90
  200.9 3.8 %all-to-all-done.2 = bf16[128,4,2,512]{3,2,1,0:T(2,128)(2,1)S(1)} async-done(((bf16[128,4,2,512]{3,2,1,0:T(2,128)(2,1)}), bf16[128,4,2,512]{3,2,1,0:T(2,128)(2,1)S(1)}, u32[]{:S(2)}, u32[]{:S(2)}) %all-to-all-start.2) | async-done | bytes 1048608 | tf_op jit(solution)/shard_map/all_to_all | solution.py:99
  204.7 1.6 fusion.3
  206.3 3.3 %all-to-all-start.3 = ((bf16[4,16,512]{2,1,0:T(8,128)(2,1)}), bf16[4,16,512]{2,1,0:T(8,128)(2,1)S(1)}, u32[]{:S(2)}, u32[]{:S(2)}) async-start(bf16[4,16,512]{2,1,0:T(8,128)(2,1)} %fusion.3), calls=%async_computation.3 | async-start | bytes 131072 | tf_op jit(solution)/shard_map/all_to_all | solution.py:108
  209.6 4.1 %fusion.1 = bf16[1,192,2048]{2,1,0:T(8,128)(2,1)} fusion(bf16[1024,2048]{1,0:T(8,128)(2,1)} %all-gather.8.cloned.1.call-done, f32[192,1024]{1,0:T(8,128)S(1)} %copy-done.7, f32[192,1024]{1,0:T(8,128)S(1)} %copy-done.9), kind=kOutput, calls=%fused_computation.4 | convolution fusion | flops 806879232 | bytes 6553600 | tf_op jit(solution)/shard_map/dot_general | solution.py:93
  (47 shorter events, 6.9 us)
Async XLA Ops:
  7.2 133.4 %copy-start = (bf16[1,768,512]{2,1,0:T(8,128)(2,1)S(1)}, bf16[1,768,512]{2,1,0:T(8,128)(2,1)}, u32[]{:S(2)}) copy-start(bf16[1,768,512]{2,1,0:T(8,128)(2,1)} %param.13) | copy-start | bytes 2359300
  7.2 103.5 %all-gather.8.cloned.1.call-start = ((), (), s32[]{:S(2)}) async-start(), calls=%async_computation.5 | async-start | bytes 5242880 | tf_op jit(solution)/shard_map/all_gather | solution.py:34
  10.6 50.5 %copy-start.3 = (f32[16,8]{0,1:T(8,128)S(1)}, f32[16,8]{0,1:T(8,128)}, u32[]{:S(2)}) copy-start(f32[16,8]{0,1:T(8,128)} %param.10) | copy-start | bytes 1540
  10.6 60.1 %copy-start.2 = (s32[16,8]{0,1:T(8,128)S(1)}, s32[16,8]{0,1:T(8,128)}, u32[]{:S(2)}) copy-start(s32[16,8]{0,1:T(8,128)} %param.9) | copy-start | bytes 1540
  10.6 70.4 %copy-start.1 = (bf16[16,2048]{1,0:T(8,128)(2,1)S(1)}, bf16[16,2048]{1,0:T(8,128)(2,1)}, u32[]{:S(2)}) copy-start(bf16[16,2048]{1,0:T(8,128)(2,1)} %param.8) | copy-start | bytes 196612
  61.1 49.5 %copy-start.5 = (bf16[1,192,2048]{2,1,0:T(8,128)(2,1)S(1)}, bf16[1,192,2048]{2,1,0:T(8,128)(2,1)}, u32[]{:S(2)}) copy-start(bf16[1,192,2048]{2,1,0:T(8,128)(2,1)} %param.11) | copy-start | bytes 2359300
  95.7 43.6 %all-to-all-start.1 = ((bf16[128,4,2,512]{3,2,1,0:T(2,128)(2,1)}), bf16[128,4,2,512]{3,2,1,0:T(2,128)(2,1)S(1)}, u32[]{:S(2)}, u32[]{:S(2)}) async-start(bf16[128,4,2,512]{3,2,1,0:T(2,128)(2,1)} %copy.39), calls=%async_computation.1 | async-start | bytes 2097152 | tf_op jit(solution)/shard_map/all_to_all | solution.py:55
  108.5 6.1 %copy-start.6 = (bf16[1,192,2048]{2,1,0:T(8,128)(2,1)S(1)}, bf16[1,192,2048]{2,1,0:T(8,128)(2,1)}, u32[]{:S(2)}) copy-start(bf16[1,192,2048]{2,1,0:T(8,128)(2,1)} %param.12) | copy-start | bytes 2359300
  108.5 41.0 %all-gather.10.cloned.1.call-start = ((), (), s32[]{:S(2)}) async-start(), calls=%async_computation.6 | async-start | bytes 1966080 | tf_op jit(solution)/shard_map/all_gather | solution.py:71
  110.7 3.9 %copy-start.4 = (bf16[1024,2048]{1,0:T(8,128)(2,1)S(1)}, bf16[1024,2048]{1,0:T(8,128)(2,1)}, u32[]{:S(2)}) copy-start(bf16[1024,2048]{1,0:T(8,128)(2,1)} %all-gather.8.cloned.1.call-done) | copy-start | bytes 12582916
  114.6 2.6 %copy-start.8 = (f32[192,1024]{1,0:T(8,128)}, f32[192,1024]{1,0:T(8,128)S(1)}, u32[]{:S(2)}) copy-start(f32[192,1024]{1,0:T(8,128)S(1)} %convolution_bitcast_fusion.2) | copy-start | bytes 2359300
  117.2 79.0 %reduce-scatter.2.cloned.1.call-start = ((), (), s32[]{:S(2)}) async-start(), calls=%async_computation.7 | async-start | bytes 3932160 | tf_op jit(solution)/shard_map/reduce_scatter | solution.py:79
  156.1 40.0 %copy-start.9 = (f32[192,1024]{1,0:T(8,128)S(1)}, f32[192,1024]{1,0:T(8,128)}, u32[]{:S(2)}) copy-start(f32[192,1024]{1,0:T(8,128)} %copy-done.8) | copy-start | bytes 2359300
  159.5 45.2 %all-to-all-start.2 = ((bf16[128,4,2,512]{3,2,1,0:T(2,128)(2,1)}), bf16[128,4,2,512]{3,2,1,0:T(2,128)(2,1)S(1)}, u32[]{:S(2)}, u32[]{:S(2)}) async-start(bf16[128,4,2,512]{3,2,1,0:T(2,128)(2,1)} %bitcast.71), calls=%async_computation.2 | async-start | bytes 2097152 | tf_op jit(solution)/shard_map/all_to_all | solution.py:99
  196.1 13.5 %copy-start.7 = (f32[192,1024]{1,0:T(8,128)S(1)}, f32[192,1024]{1,0:T(8,128)}, u32[]{:S(2)}) copy-start(f32[192,1024]{1,0:T(8,128)} %reduce-scatter.2.cloned.1.call-done) | copy-start | bytes 2359300
  206.3 7.7 %all-to-all-start.3 = ((bf16[4,16,512]{2,1,0:T(8,128)(2,1)}), bf16[4,16,512]{2,1,0:T(8,128)(2,1)S(1)}, u32[]{:S(2)}, u32[]{:S(2)}) async-start(bf16[4,16,512]{2,1,0:T(8,128)(2,1)} %fusion.3), calls=%async_computation.3 | async-start | bytes 131072 | tf_op jit(solution)/shard_map/all_to_all | solution.py:108
Sparse Core Ops, SparseCore 0:
  61.3 49.3 all-gather.7
  117.3 32.1 all-gather.9
  152.3 43.7 reduce-scatter.1

commit v8 on v1

--- a/solution.py
+++ b/solution.py
@@ -35,8 +35,11 @@
         arrived_input.reshape(experts * capacity, width), "dp", axis=0, tiled=True
     )
 
-    col_routes = lax.all_gather(routes, "dp", axis=0, tiled=False)
-    col_gates = lax.all_gather(gate_values, "dp", axis=0, tiled=False)
+    col_meta = lax.all_gather(
+        jnp.concatenate([routes.astype(jnp.float32), gate_values], axis=1), "dp", axis=0, tiled=False
+    )
+    col_routes = col_meta[:, :, :top_count].astype(jnp.int32)
+    col_gates = col_meta[:, :, top_count:]
     col_cot = lax.all_gather(cotangent, "dp", axis=0, tiled=False)
     me = lax.axis_index("dp")
     cot_q = lax.dynamic_slice_in_dim(col_cot, me * quarter, quarter, axis=2)

time: 220 us -> 219 us (level)
  waiting for transfers between devices: 57.3 us -> 67.9 us
  blocking collectives: 80.6 us -> 70.3 us
    all_to_all x1, waiting for transfers between devices: 21.9 us -> 10 us  [body(): lax.all_to_all(row_cot, 'expert', split_axis=0, concat_axis=0, tiled=True)]
    all_gather x1, waiting for transfers between devices: 2.14 us -> 14.1 us  [body(): lax.all_gather(arrived_input.reshape(experts * capacity, width), 'dp', ax...]
    all_gather x1, waiting for transfers between devices: 6.24 us -> 16.9 us  [body(): hidden_all = lax.all_gather(hidden_part, 'dp', axis=0, tiled=True)]
    all_gather x2 -> x1, blocking collectives: 19.5 us -> 9.61 us  [body(): lax.all_gather(jnp.concatenate([routes.astype(jnp.float32), gate_values],...]
where the time goes in v8:
time: 219 us; the launch traced here: 218 us
  blocking collectives  70.3 us (32%)
  waiting for transfers between devices  67.9 us (31%)
  starting transfers between devices  28.8 us (13%)
  matrix products  26 us (12%)
  between operations  14 us (6%)
  local copies, waits for them, and re-layouts  10.4 us (5%)
    all_to_all x1, blocking collectives, body(): lax.all_to_all(row_input, 'expert', split_axis=0, concat_axis=0, tiled=True)  49.3 us
    reduce_scatter x1, waiting for transfers between devices, body(): lax.psum_scatter(lax.dot_general(down_local, cot_quarter, contract_last,...  25.8 us
    all_gather x1, waiting for transfers between devices, body(): hidden_all = lax.all_gather(hidden_part, 'dp', axis=0, tiled=True)  16.9 us
    all_to_all x1, starting transfers between devices, body(): lax.all_to_all(out_blocks, 'expert', split_axis=0, concat_axis=0, tiled=T...  14.3 us
    all_gather x1, waiting for transfers between devices, body(): lax.all_gather(arrived_input.reshape(experts * capacity, width), 'dp', ax...  14.1 us
    all_gather x1, blocking collectives, body(): col_cot = lax.all_gather(cotangent, 'dp', axis=0, tiled=False)  11.4 us
    all_to_all x1, starting transfers between devices, body(): lax.all_to_all(row_cot, 'expert', split_axis=0, concat_axis=0, tiled=True)  11 us
    all_to_all x1, waiting for transfers between devices, body(): lax.all_to_all(row_cot, 'expert', split_axis=0, concat_axis=0, tiled=True)  10 us
  transfers between devices with their start and end apart: 6, of which 5 were waited for; matrix products, arithmetic and copies ran while one was open for 14% of the time, Pallas kernels for 0%

profile of v8, /device:TPU:1, one launch (start us, length us, event | category | flops | bytes accessed | tf_op | source)
XLA Modules:
  0.0 218.1 jit_solution(7028692347580004994)
XLA Ops:
  8.2 1.3 convolution_convert_fusion
  10.6 49.3 %all_to_all.30 = bf16[128,2,2048]{2,1,0:T(2,128)(2,1)S(1)} all-to-all(bf16[128,2,2048]{2,1,0:T(2,128)(2,1)S(1)} %copy.46), channel_id=1, replica_groups=mesh['dp'=4,'expert'=128] {'expert'}, dimensions={0} | all-to-all | bytes 2097152 | tf_op jit(solution)/shard_map/all_to_all | solution.py:33
  59.9 1.2 reshape.30
  61.2 9.6 %all-gather = f32[64,16]{1,0:T(8,128)S(1)} all-gather(f32[16,16]{1,0:T(8,128)S(1)} %copy.44), channel_id=2, replica_groups=mesh['dp'=4,'expert'=128] {'dp'}, dimensions={0}, use_global_device_ids=true | all-gather | bytes 5120 | tf_op jit(solution)/shard_map/all_gather | solution.py:38
  71.1 11.4 %all-gather.1 = bf16[64,2048]{1,0:T(8,128)(2,1)S(1)} all-gather(bf16[16,2048]{1,0:T(8,128)(2,1)S(1)} %copy-done.1), channel_id=3, replica_groups=mesh['dp'=4,'expert'=128] {'dp'}, dimensions={0}, use_global_device_ids=true | all-gather | bytes 327680 | tf_op jit(solution)/shard_map/all_gather | solution.py:43
  83.3 2.1 copy.50
  85.4 11.0 %all-to-all-start.3 = ((bf16[128,4,2,512]{3,2,1,0:T(2,128)(2,1)}), bf16[128,4,2,512]{3,2,1,0:T(2,128)(2,1)S(1)}, u32[]{:S(2)}, u32[]{:S(2)}) async-start(bf16[128,4,2,512]{3,2,1,0:T(2,128)(2,1)} %copy.50), calls=%async_computation.3 | async-start | bytes 2097152 | tf_op jit(solution)/shard_map/all_to_all | solution.py:58
  96.4 14.1 %all-gather.5.cloned.1.call-done = bf16[1024,2048]{1,0:T(8,128)(2,1)} async-done(((bf16[256,2048]{1,0:T(8,128)(2,1)}), bf16[1024,2048]{1,0:T(8,128)(2,1)}) %all-gather.5.cloned.1.call-update) | async-done | bytes 4194320 | tf_op jit(solution)/shard_map/all_gather | solution.py:34
  110.5 3.9 %convolution_bitcast_fusion.2 = f32[192,1024]{1,0:T(8,128)S(1)} fusion(bf16[1024,2048]{1,0:T(8,128)(2,1)} %all-gather.5.cloned.1.call-done, bf16[1,192,2048]{2,1,0:T(8,128)(2,1)S(1)} %copy-done.6), kind=kOutput, calls=%fused_computation.12 | convolution fusion | flops 805306368 | bytes 5767168 | tf_op jit(solution)/shard_map/dot_general | solution.py:67
  114.4 2.6 %multiply_convert_fusion.2 = (bf16[192,1024]{1,0:T(8,128)(2,1)}, f32[192,1024]{1,0:T(8,128)}) fusion(f32[192,1024]{1,0:T(8,128)S(1)} %convolution_bitcast_fusion.2, bf16[1024,2048]{1,0:T(8,128)(2,1)S(1)} %copy-done.4, bf16[1,192,2048]{2,1,0:T(8,128)(2,1)S(1)} %copy-done.7), kind=kOutput, calls=%fused_computation.23 | convolution fusion | flops 806486016 | bytes 6946816 | tf_op jit(solution)/shard_map/dot_general | solution.py:70
  117.3 10.0 %all-to-all-done.3 = bf16[128,4,2,512]{3,2,1,0:T(2,128)(2,1)S(1)} async-done(((bf16[128,4,2,512]{3,2,1,0:T(2,128)(2,1)}), bf16[128,4,2,512]{3,2,1,0:T(2,128)(2,1)S(1)}, u32[]{:S(2)}, u32[]{:S(2)}) %all-to-all-start.3) | async-done | bytes 1048608 | tf_op jit(solution)/shard_map/all_to_all | solution.py:58
  128.5 2.7 %convolution_bitcast_fusion = f32[768,1024]{1,0:T(8,128)} fusion(bf16[1024,512]{1,0:T(8,128)(2,1)S(1)} %reshape.32, bf16[1,768,512]{2,1,0:T(8,128)(2,1)S(1)} %copy-done), kind=kOutput, calls=%fused_computation.7 | convolution fusion | flops 805306368 | bytes 4980736 | tf_op jit(solution)/shard_map/dot_general | solution.py:83
  131.2 16.9 %all-gather.7.cloned.1.call-done = bf16[768,1024]{1,0:T(8,128)(2,1)} async-done(((bf16[192,1024]{1,0:T(8,128)(2,1)}), bf16[768,1024]{1,0:T(8,128)(2,1)}) %all-gather.7.cloned.1.call-update) | async-done | bytes 1572880 | tf_op jit(solution)/shard_map/all_gather | solution.py:74
  148.0 3.4 %convolution_convert_fusion.3 = bf16[1024,512]{1,0:T(8,128)(2,1)} fusion(bf16[768,1024]{1,0:T(8,128)(2,1)} %all-gather.7.cloned.1.call-done, bf16[1,768,512]{2,1,0:T(8,128)(2,1)S(1)} %copy-done), kind=kOutput, calls=%fused_computation.8 | convolution fusion | flops 805830656 | bytes 3407872 | tf_op jit(solution)/shard_map/dot_general | solution.py:76
  151.4 1.5 reshape.31
  152.9 1.7 copy.60
  154.6 14.3 %all-to-all-start.1 = ((bf16[128,4,2,512]{3,2,1,0:T(2,128)(2,1)}), bf16[128,4,2,512]{3,2,1,0:T(2,128)(2,1)S(1)}, u32[]{:S(2)}, u32[]{:S(2)}) async-start(bf16[128,4,2,512]{3,2,1,0:T(2,128)(2,1)} %bitcast.73), calls=%async_computation.1 | async-start | bytes 2097152 | tf_op jit(solution)/shard_map/all_to_all | solution.py:101
  168.9 25.8 %reduce-scatter.2.cloned.1.call-done = f32[192,1024]{1,0:T(8,128)} async-done(((f32[768,1024]{1,0:T(8,128)}), f32[192,1024]{1,0:T(8,128)}) %reduce-scatter.2.cloned.1.call-update) | async-done | bytes 786448 | tf_op jit(solution)/shard_map/reduce_scatter | solution.py:82
  194.7 4.7 %fusion.1 = bf16[1,192,2048]{2,1,0:T(8,128)(2,1)} fusion(bf16[1024,2048]{1,0:T(8,128)(2,1)} %all-gather.5.cloned.1.call-done, f32[192,1024]{1,0:T(8,128)} %reduce-scatter.2.cloned.1.call-done, f32[192,1024]{1,0:T(8,128)} %copy-done.9), kind=kOutput, calls=%fused_computation.4 | convolution fusion | flops 806879232 | bytes 6553600 | tf_op jit(solution)/shard_map/dot_general | solution.py:96
  199.4 2.0 fusion
  201.5 1.6 fusion.4
  203.1 3.3 %all-to-all-start.2 = ((bf16[4,16,512]{2,1,0:T(8,128)(2,1)}), bf16[4,16,512]{2,1,0:T(8,128)(2,1)S(1)}, u32[]{:S(2)}, u32[]{:S(2)}) async-start(bf16[4,16,512]{2,1,0:T(8,128)(2,1)} %fusion.4), calls=%async_computation.2 | async-start | bytes 131072 | tf_op jit(solution)/shard_map/all_to_all | solution.py:110
  206.4 3.3 %fusion.3 = bf16[1,768,512]{2,1,0:T(8,128)(2,1)} fusion(bf16[768,1024]{1,0:T(8,128)(2,1)} %all-gather.7.cloned.1.call-done, bf16[1024,512]{1,0:T(8,128)(2,1)S(1)} %reshape.32), kind=kOutput, calls=%fused_computation.10 | convolution fusion | flops 805699584 | bytes 3407872 | tf_op jit(solution)/shard_map/dot_general | solution.py:79
  209.7 1.2 all-to-all-done.2
  (52 shorter events, 5.4 us)
Async XLA Ops:
  7.2 121.3 %copy-start = (bf16[1,768,512]{2,1,0:T(8,128)(2,1)S(1)}, bf16[1,768,512]{2,1,0:T(8,128)(2,1)}, u32[]{:S(2)}) copy-start(bf16[1,768,512]{2,1,0:T(8,128)(2,1)} %param.13) | copy-start | bytes 2359300
  7.2 103.3 %all-gather.5.cloned.1.call-start = ((), (), s32[]{:S(2)}) async-start(), calls=%async_computation.5 | async-start | bytes 5242880 | tf_op jit(solution)/shard_map/all_gather | solution.py:34
  10.6 50.5 %copy-start.2 = (s32[16,8]{0,1:T(8,128)S(1)}, s32[16,8]{0,1:T(8,128)}, u32[]{:S(2)}) copy-start(s32[16,8]{0,1:T(8,128)} %param.9) | copy-start | bytes 1540
  10.6 50.5 %copy-start.3 = (f32[16,8]{0,1:T(8,128)S(1)}, f32[16,8]{0,1:T(8,128)}, u32[]{:S(2)}) copy-start(f32[16,8]{0,1:T(8,128)} %param.10) | copy-start | bytes 1540
  10.6 60.5 %copy-start.1 = (bf16[16,2048]{1,0:T(8,128)(2,1)S(1)}, bf16[16,2048]{1,0:T(8,128)(2,1)}, u32[]{:S(2)}) copy-start(bf16[16,2048]{1,0:T(8,128)(2,1)} %param.8) | copy-start | bytes 196612
  70.8 39.7 %copy-start.6 = (bf16[1,192,2048]{2,1,0:T(8,128)(2,1)S(1)}, bf16[1,192,2048]{2,1,0:T(8,128)(2,1)}, u32[]{:S(2)}) copy-start(bf16[1,192,2048]{2,1,0:T(8,128)(2,1)} %param.11) | copy-start | bytes 2359300
  85.4 41.9 %all-to-all-start.3 = ((bf16[128,4,2,512]{3,2,1,0:T(2,128)(2,1)}), bf16[128,4,2,512]{3,2,1,0:T(2,128)(2,1)S(1)}, u32[]{:S(2)}, u32[]{:S(2)}) async-start(bf16[128,4,2,512]{3,2,1,0:T(2,128)(2,1)} %copy.50), calls=%async_computation.3 | async-start | bytes 2097152 | tf_op jit(solution)/shard_map/all_to_all | solution.py:58
  96.4 18.0 %copy-start.7 = (bf16[1,192,2048]{2,1,0:T(8,128)(2,1)S(1)}, bf16[1,192,2048]{2,1,0:T(8,128)(2,1)}, u32[]{:S(2)}) copy-start(bf16[1,192,2048]{2,1,0:T(8,128)(2,1)} %param.12) | copy-start | bytes 2359300
  96.4 51.6 %all-gather.7.cloned.1.call-start = ((), (), s32[]{:S(2)}) async-start(), calls=%async_computation.6 | async-start | bytes 1966080 | tf_op jit(solution)/shard_map/all_gather | solution.py:74
  110.5 3.9 %copy-start.4 = (bf16[1024,2048]{1,0:T(8,128)(2,1)S(1)}, bf16[1024,2048]{1,0:T(8,128)(2,1)}, u32[]{:S(2)}) copy-start(bf16[1024,2048]{1,0:T(8,128)(2,1)} %all-gather.5.cloned.1.call-done) | copy-start | bytes 12582916
  114.4 2.6 %copy-start.9 = (f32[192,1024]{1,0:T(8,128)}, f32[192,1024]{1,0:T(8,128)S(1)}, u32[]{:S(2)}) copy-start(f32[192,1024]{1,0:T(8,128)S(1)} %convolution_bitcast_fusion.2) | copy-start | bytes 2359300
  117.0 77.6 %reduce-scatter.2.cloned.1.call-start = ((), (), s32[]{:S(2)}) async-start(), calls=%async_computation.7 | async-start | bytes 3932160 | tf_op jit(solution)/shard_map/reduce_scatter | solution.py:82
  154.6 46.8 %all-to-all-start.1 = ((bf16[128,4,2,512]{3,2,1,0:T(2,128)(2,1)}), bf16[128,4,2,512]{3,2,1,0:T(2,128)(2,1)S(1)}, u32[]{:S(2)}, u32[]{:S(2)}) async-start(bf16[128,4,2,512]{3,2,1,0:T(2,128)(2,1)} %bitcast.73), calls=%async_computation.1 | async-start | bytes 2097152 | tf_op jit(solution)/shard_map/all_to_all | solution.py:101
  194.7 4.7 %copy-start.5 = (bf16[1024,2048]{1,0:T(8,128)(2,1)S(1)}, bf16[1024,2048]{1,0:T(8,128)(2,1)}, u32[]{:S(2)}) copy-start(bf16[1024,2048]{1,0:T(8,128)(2,1)} %all-gather.5.cloned.1.call-done) | copy-start | bytes 12582916
  194.7 4.7 %copy-start.8 = (f32[192,1024]{1,0:T(8,128)S(1)}, f32[192,1024]{1,0:T(8,128)}, u32[]{:S(2)}) copy-start(f32[192,1024]{1,0:T(8,128)} %reduce-scatter.2.cloned.1.call-done) | copy-start | bytes 2359300
  194.7 4.7 %copy-start.10 = (f32[192,1024]{1,0:T(8,128)S(1)}, f32[192,1024]{1,0:T(8,128)}, u32[]{:S(2)}) copy-start(f32[192,1024]{1,0:T(8,128)} %copy-done.9) | copy-start | bytes 2359300
  194.7 4.7 %copy-start.11 = (f32[192,1024]{1,0:T(8,128)S(1)}, f32[192,1024]{1,0:T(8,128)}, u32[]{:S(2)}) copy-start(f32[192,1024]{1,0:T(8,128)} %get-tuple-element.7) | copy-start | bytes 2359300
  203.1 7.7 %all-to-all-start.2 = ((bf16[4,16,512]{2,1,0:T(8,128)(2,1)}), bf16[4,16,512]{2,1,0:T(8,128)(2,1)S(1)}, u32[]{:S(2)}, u32[]{:S(2)}) async-start(bf16[4,16,512]{2,1,0:T(8,128)(2,1)} %fusion.4), calls=%async_computation.2 | async-start | bytes 131072 | tf_op jit(solution)/shard_map/all_to_all | solution.py:110
Sparse Core Ops, SparseCore 0:
  61.2 49.2 all-gather.4
  117.2 30.8 all-gather.6
  150.9 43.7 reduce-scatter.1
